TPU v7x, 32 devices: a whole 2x2x4 slice. The times are simulated.
32 devices in a mesh: dp: 8 (over z, y), mp: 4 (over x, core).
Axes of the slice: x: 2, y: 2, z: 4, core: 2. Of those that a mesh axis runs over, the one named last changes fastest.
Arguments:
- ids: int32 [8192], P('dp'), may hold values from 0 to 16777215, as said below
- hash_a: int32 [1024], replicated, may hold values from 1 to 16383
- hash_b: int32 [1024], replicated, may hold values from 0 to 16383
- hash_p: int32 [1024], replicated, may hold values from 16384 to 32767
- hash_m: int32 [1024], replicated, may hold values from 4096 to 16383
- w_in: bfloat16 [1024, 2048], P(None, 'mp'), may hold values from -0.1875 to 0.1875
- w_mid: bfloat16 [2, 2048, 2048], P(None, None, 'mp'), may hold values from -0.125 to 0.125
- w_out: bfloat16 [2048, 64], P('mp'), may hold values from -0.125 to 0.125
- bn_gain: float32 [3, 2048], P(None, 'mp'), may hold values from 0.25 to 1.75
- bn_bias: float32 [3, 2048], P(None, 'mp'), may hold values from -3 to 3
- target: float32 [8192, 64], P('dp'), may hold values from -6 to 6
Outputs:
- grad_w_in: float32 [1024, 2048], P('dp', 'mp')
- grad_w_mid: float32 [2, 2048, 2048], P(None, 'dp', 'mp')
- grad_w_out: float32 [2048, 64], P(('mp', 'dp'))
- grad_gain: float32 [3, 2048], P(None, 'mp')
- grad_bias: float32 [3, 2048], P(None, 'mp')
Inputs may be any that keep to these rules, and one draw needn't show every extreme that they name: The number of distinct ids among one device's 1024 rows differs from device to device, from one to many.
All inputs are finite; a program needn't handle non-finite values.
Results may differ from a plain program's by a relative error of at most 0.02.
Values may be sent and summed in bfloat16 or wider, within the bound.
A program may use at most 128 MiB of HBM per device.

v0:
```python
import math

import jax
import jax.numpy as jnp
from jax import lax
from jax.sharding import PartitionSpec as P

epsilon_norm = 1e-05


def encode(ids, hash_a, hash_b, hash_p, hash_m):
    reduced = ids[:, None] % hash_p[None, :]
    hashed = (hash_a[None, :] * reduced + hash_b[None, :]) % hash_p[None, :] % hash_m[None, :]
    scaled = 2.0 * hashed.astype(jnp.float32) / (hash_m[None, :] - 1).astype(jnp.float32) - 1.0
    return scaled.astype(jnp.bfloat16)


def mish_act(values):
    return values * jnp.tanh(jax.nn.softplus(values))


def mish_slope(values):
    tangent = jnp.tanh(jax.nn.softplus(values))
    return tangent + values * (1.0 - tangent * tangent) * jax.nn.sigmoid(values)


def column_stats(summed, batch_total):
    totals, squares = lax.psum((jnp.sum(summed, axis=0), jnp.sum(summed * summed, axis=0)), "dp")
    average = totals / batch_total
    spread = squares / batch_total - average * average
    centered = summed - average
    inverse = 1.0 / jnp.sqrt(spread + epsilon_norm)
    return (centered * inverse, inverse)


def column_products(left_rows, right_rows):
    return jnp.dot(left_rows.T, right_rows, preferred_element_type=jnp.float32)


def per_device(ids, hash_a, hash_b, hash_p, hash_m, w_in, w_mid, w_out, bn_gain, bn_bias, target):
    batch_devices = lax.axis_size("dp")
    batch_total = ids.shape[0] * batch_devices
    layer_count = bn_gain.shape[0]
    encoded = encode(ids, hash_a, hash_b, hash_p, hash_m)
    full_inputs = []
    saved = []
    current = encoded
    for layer_at in range(layer_count):
        if layer_at == 0:
            whole_input = encoded
            summed = jnp.dot(whole_input, w_in, preferred_element_type=jnp.float32)
        else:
            whole_input = lax.all_gather(current, "mp", axis=1, tiled=True)
            summed = jnp.dot(whole_input, w_mid[layer_at - 1], preferred_element_type=jnp.float32)
        full_inputs.append(whole_input)
        normed, inverse = column_stats(summed, batch_total)
        shifted = bn_gain[layer_at] * normed + bn_bias[layer_at]
        current = mish_act(shifted).astype(jnp.bfloat16)
        saved.append((normed, inverse, shifted))
    partial_out = jnp.dot(current, w_out, preferred_element_type=jnp.float32)
    predicted = lax.psum(partial_out.astype(jnp.bfloat16), "mp").astype(jnp.float32)
    residual_out = ((predicted - target) / math.sqrt(batch_total)).astype(jnp.bfloat16)
    grad_out = lax.psum_scatter(
        column_products(current, residual_out).astype(jnp.bfloat16),
        "dp",
        scatter_dimension=0,
        tiled=True,
    ).astype(jnp.float32)
    upstream = jnp.dot(residual_out, w_out.T, preferred_element_type=jnp.float32)
    grads_gain = []
    grads_bias = []
    grads_mid = []
    grad_first = None
    for layer_at in reversed(range(layer_count)):
        normed, inverse, shifted = saved[layer_at]
        slope_a = upstream * mish_slope(shifted)
        bias_sum, gain_sum = lax.psum(
            (jnp.sum(slope_a, axis=0), jnp.sum(slope_a * normed, axis=0)), "dp"
        )
        slope_z = (
            bn_gain[layer_at]
            * inverse
            * (slope_a - bias_sum / batch_total - normed * gain_sum / batch_total)
        ).astype(jnp.bfloat16)
        whole_input = full_inputs[layer_at]
        if layer_at == 0:
            grad_first = lax.psum_scatter(
                column_products(whole_input, slope_z).astype(jnp.bfloat16),
                "dp",
                scatter_dimension=0,
                tiled=True,
            ).astype(jnp.float32)
        else:
            grads_mid.append(
                lax.psum_scatter(
                    column_products(whole_input, slope_z).astype(jnp.bfloat16),
                    "dp",
                    scatter_dimension=0,
                    tiled=True,
                ).astype(jnp.float32)
            )
            weights = w_mid[layer_at - 1]
            partial_in = jnp.dot(slope_z, weights.T, preferred_element_type=jnp.float32)
            upstream = lax.psum_scatter(
                partial_in.astype(jnp.bfloat16), "mp", scatter_dimension=1, tiled=True
            ).astype(jnp.float32)
        grads_gain.append(gain_sum)
        grads_bias.append(bias_sum)
    grad_mid = jnp.stack(grads_mid[::-1])
    grad_gain = jnp.stack(grads_gain[::-1])
    grad_bias = jnp.stack(grads_bias[::-1])
    return (grad_first, grad_mid, grad_out, grad_gain, grad_bias)


def solution(mesh):
    return jax.shard_map(
        per_device,
        mesh=mesh,
        in_specs=(
            P("dp"),
            P(),
            P(),
            P(),
            P(),
            P(None, "mp"),
            P(None, None, "mp"),
            P("mp", None),
            P(None, "mp"),
            P(None, "mp"),
            P("dp", None),
        ),
        out_specs=(
            P("dp", "mp"),
            P(None, "dp", "mp"),
            P(("mp", "dp"), None),
            P(None, "mp"),
            P(None, "mp"),
        ),
        check_vma=False,
    )
```

profile of v0, /device:TPU:0, one launch (start us, length us, event | category | flops | bytes accessed | tf_op | source)
XLA Modules:
  0.0 749.5 jit_solution(10911599320703167918)
XLA Ops:
  7.2 0.0 all-gather.3.cloned.1.call-start
  7.2 0.8 broadcast_compare_fusion
  8.0 0.8 fusion.55
  8.8 0.8 fusion.56
  9.6 0.7 compare_select_fusion.5
  10.3 0.7 compare_reduce_fusion
  11.1 125.3 %fusion.54 = (f32[512]{0:T(512)S(1)}, f32[512]{0:T(512)S(1)}, f32[1024,512]{1,0:T(8,128)S(1)}) fusion(bf16[1024,512]{1,0:T(8,128)(2,1)S(1)} %copy-done, s32[1024]{0:T(1024)S(1)} %bitcast.69, s32[1024]{0:T(1024)S(1)} %bitcast.71, f32[1024]{0:T(1024)S(1)} %get-tuple-element.58, s32[1024]{0:T(1024)} %param.15, s32[1024]{0:T(1024)S(1)} %get-tuple-element.57, ...), kind=kOutput, calls=%fused_computation.109 | convolution fusion | flops 1104673792 | bytes 3181568 | tf_op jit(solution)/shard_map/dot_general | solution.py:51
  136.5 23.2 %all-reduce.5 = (f32[512]{0:T(512)S(1)}, f32[512]{0:T(512)S(1)}) all-reduce(f32[512]{0:T(512)S(1)} %get-tuple-element.17, f32[512]{0:T(512)S(1)} %get-tuple-element.16), channel_id=1, replica_groups=mesh['dp'=8,'mp'=4] {'dp'}, use_global_device_ids=true, to_apply=%region_1.3 | all-reduce | flops 1024 | bytes 8192 | tf_op jit(solution)/shard_map/psum | solution.py:28
  159.6 0.6 fusion.41
  160.2 2.5 fusion.21
  162.8 0.0 all-gather.3.cloned.1.call-update
  162.8 0.0 all-gather.5.cloned.1.call-start
  162.8 31.8 %all-gather.3.cloned.1.call-done = bf16[1024,2048]{1,0:T(8,128)(2,1)} async-done(((bf16[1024,512]{1,0:T(8,128)(2,1)}), bf16[1024,2048]{1,0:T(8,128)(2,1)}) %all-gather.3.cloned.1.call-update) | async-done | bytes 4194320 | tf_op jit(solution)/shard_map/all_gather | solution.py:53
  194.6 5.2 fusion.53
  199.9 21.5 %all-reduce.4 = (f32[512]{0:T(512)S(1)}, f32[512]{0:T(512)S(1)}) all-reduce(f32[512]{0:T(512)S(1)} %get-tuple-element.15, f32[512]{0:T(512)S(1)} %get-tuple-element.14), channel_id=1, replica_groups=mesh['dp'=8,'mp'=4] {'dp'}, use_global_device_ids=true, to_apply=%region_5.7 | all-reduce | flops 1024 | bytes 8192 | tf_op jit(solution)/shard_map/psum | solution.py:28
  221.4 2.5 fusion.23
  223.9 0.0 all-gather.5.cloned.1.call-update
  223.9 0.0 all-reduce.8.cloned.1.call-start
  224.0 30.9 %all-gather.5.cloned.1.call-done = bf16[1024,2048]{1,0:T(8,128)(2,1)} async-done(((bf16[1024,512]{1,0:T(8,128)(2,1)}), bf16[1024,2048]{1,0:T(8,128)(2,1)}) %all-gather.5.cloned.1.call-update) | async-done | bytes 4194320 | tf_op jit(solution)/shard_map/all_gather | solution.py:53
  254.9 6.6 fusion.52
  261.4 21.5 %all-reduce.3 = (f32[512]{0:T(512)S(1)}, f32[512]{0:T(512)S(1)}) all-reduce(f32[512]{0:T(512)S(1)} %get-tuple-element.13, f32[512]{0:T(512)S(1)} %get-tuple-element.12), channel_id=1, replica_groups=mesh['dp'=8,'mp'=4] {'dp'}, use_global_device_ids=true, to_apply=%region_9.11 | all-reduce | flops 1024 | bytes 8192 | tf_op jit(solution)/shard_map/psum | solution.py:28
  282.9 3.2 fusion.25
  286.1 1.0 copy-done.1
  287.1 1.1 convolution_convert_fusion.5
  288.2 0.0 all-reduce.8.cloned.1.call-update
  288.2 0.0 reduce-scatter.7.cloned.1.call-start
  288.3 28.2 %all-reduce.8.cloned.1.call-done = bf16[1024,64]{0,1:T(8,128)(2,1)} async-done(((bf16[1024,64]{0,1:T(8,128)(2,1)}), bf16[1024,64]{0,1:T(8,128)(2,1)}) %all-reduce.8.cloned.1.call-update) | async-done | bytes 131088 | tf_op jit(solution)/shard_map/psum | solution.py:61
  316.5 5.5 fusion.51
  321.9 21.3 %all-reduce.2 = (f32[512]{0:T(512)S(1)}, f32[512]{0:T(512)S(1)}) all-reduce(f32[512]{0:T(512)S(1)} %get-tuple-element.11, f32[512]{0:T(512)S(1)} %get-tuple-element.10), channel_id=1, replica_groups=mesh['dp'=8,'mp'=4] {'dp'}, use_global_device_ids=true, to_apply=%region_16.18 | all-reduce | flops 1024 | bytes 8192 | tf_op jit(solution)/shard_map/psum | solution.py:77
  343.3 3.0 multiply_convert_fusion.2
  346.3 1.0 copy-done.5
  347.3 4.3 convolution_convert_fusion.1
  351.6 0.0 reduce-scatter.7.cloned.1.call-update
  351.6 0.3 reduce-scatter.9.cloned.1.call-start
  351.9 40.5 %reduce-scatter.7.cloned.1.call-done = bf16[1024,512]{1,0:T(8,128)(2,1)} async-done(((bf16[1024,2048]{1,0:T(8,128)(2,1)}), bf16[1024,512]{1,0:T(8,128)(2,1)}) %reduce-scatter.7.cloned.1.call-update) | async-done | bytes 1048592 | tf_op jit(solution)/shard_map/reduce_scatter | solution.py:104
  392.4 5.0 fusion.50
  397.4 21.4 %all-reduce.1 = (f32[512]{0:T(512)S(1)}, f32[512]{0:T(512)S(1)}) all-reduce(f32[512]{0:T(512)S(1)} %get-tuple-element.9, f32[512]{0:T(512)S(1)} %get-tuple-element.8), channel_id=1, replica_groups=mesh['dp'=8,'mp'=4] {'dp'}, use_global_device_ids=true, to_apply=%region_21.23 | all-reduce | flops 1024 | bytes 8192 | tf_op jit(solution)/shard_map/psum | solution.py:77
  418.8 2.3 multiply_convert_fusion.1
  421.1 1.0 copy-done.7
  422.2 4.3 convolution_convert_fusion
  426.5 0.0 reduce-scatter.9.cloned.1.call-update
  426.5 0.0 reduce-scatter.17.cloned.1.call-start
  426.6 1.1 copy-done.2
  427.7 1.1 convolution_convert_fusion.6
  428.9 0.0 reduce-scatter.15.cloned.1.call-start
  428.9 6.3 convolution_convert_fusion.2
  435.3 0.0 reduce-scatter.15.cloned.1.call-update
  435.3 0.0 reduce-scatter.13.cloned.1.call-start
  435.3 1.1 copy-done.8
  436.5 5.9 convolution_convert_fusion.3
  442.5 0.0 reduce-scatter.11.cloned.1.call-start
  442.6 24.8 %reduce-scatter.9.cloned.1.call-done = bf16[1024,512]{1,0:T(8,128)(2,1)} async-done(((bf16[1024,2048]{1,0:T(8,128)(2,1)}), bf16[1024,512]{1,0:T(8,128)(2,1)}) %reduce-scatter.9.cloned.1.call-update) | async-done | bytes 1048592 | tf_op jit(solution)/shard_map/reduce_scatter | solution.py:104
  467.4 4.9 fusion.49
  472.4 21.8 %all-reduce = (f32[512]{0:T(512)S(1)}, f32[512]{0:T(512)S(1)}) all-reduce(f32[512]{0:T(512)S(1)} %get-tuple-element.7, f32[512]{0:T(512)S(1)} %get-tuple-element.6), channel_id=1, replica_groups=mesh['dp'=8,'mp'=4] {'dp'}, use_global_device_ids=true, to_apply=%region_26.28 | all-reduce | flops 1024 | bytes 8192 | tf_op jit(solution)/shard_map/psum | solution.py:77
  494.3 126.9 %convolution_convert_fusion.4 = bf16[1024,512]{1,0:T(8,128)(2,1)} fusion(f32[1024,512]{1,0:T(8,128)} %get-tuple-element.30, f32[1024,512]{1,0:T(8,128)S(1)} %copy-done.4, f32[512]{0:T(512)S(1)} %get-tuple-element.18, f32[512]{0:T(512)S(1)} %broadcast_multiply_fusion, f32[512]{0:T(512)S(1)} %get-tuple-element.43, f32[512]{0:T(512)S(1)} %get-tuple-element.48, ...), kind=kOutput, calls=%fused_computation.64 | convolution fusion | flops 1107820544 | bytes 5284864 | tf_op jit(solution)/shard_map/dot_general | solution.py:37
  621.2 0.0 reduce-scatter.11.cloned.1.call-update
  621.2 0.0 reduce-scatter.17.cloned.1.call-done
  621.3 1.3 convert_element_type.90
  622.6 52.0 %reduce-scatter.13.cloned.1.call-done = bf16[256,512]{1,0:T(8,128)(2,1)} async-done(((bf16[2048,512]{1,0:T(8,128)(2,1)}), bf16[256,512]{1,0:T(8,128)(2,1)}) %reduce-scatter.13.cloned.1.call-update) | async-done | bytes 262160 | tf_op jit(solution)/shard_map/reduce_scatter | solution.py:95
  674.6 2.1 maximum_convert_fusion
  676.7 0.6 pad_maximum_fusion.1
  677.3 0.6 pad_maximum_fusion
  677.9 63.3 %reduce-scatter.11.cloned.1.call-done = bf16[128,512]{1,0:T(8,128)(2,1)} async-done(((bf16[1024,512]{1,0:T(8,128)(2,1)}), bf16[128,512]{1,0:T(8,128)(2,1)}) %reduce-scatter.11.cloned.1.call-update) | async-done | bytes 131088 | tf_op jit(solution)/shard_map/reduce_scatter | solution.py:87
  741.2 1.6 convert_element_type.86
  (83 shorter events, 0.2 us)
Async XLA Ops:
  7.2 4.0 copy-start
  7.2 187.5 %all-gather.3.cloned.1.call-start = ((), (), s32[]{:S(2)}) async-start(), calls=%async_computation.6 | async-start | bytes 5242880 | tf_op jit(solution)/shard_map/all_gather | solution.py:53
  8.0 128.4 %copy-start.29 = (pred[1024]{0:T(1024)(128)(4,1)}, pred[1024]{0:T(1024)(128)(4,1)S(1)}, u32[]{:S(2)}) copy-start(pred[1024]{0:T(1024)(128)(4,1)S(1)} %broadcast_compare_fusion) | copy-start | bytes 3076
  10.3 126.1 %copy-start.20 = (s32[1024]{0:T(1024)}, s32[1024]{0:T(1024)S(1)}, u32[]{:S(2)}) copy-start(s32[1024]{0:T(1024)S(1)} %get-tuple-element.57) | copy-start | bytes 12292
  10.3 126.1 %copy-start.22 = (f32[1024]{0:T(1024)}, f32[1024]{0:T(1024)S(1)}, u32[]{:S(2)}) copy-start(f32[1024]{0:T(1024)S(1)} %get-tuple-element.58) | copy-start | bytes 12292
  11.1 125.3 %copy-start.24 = (s32[1,1024]{1,0:T(1,128)}, s32[1,1024]{1,0:T(1,128)S(1)}, u32[]{:S(2)}) copy-start(s32[1,1024]{1,0:T(1,128)S(1)} %get-tuple-element.35) | copy-start | bytes 12292
  11.1 125.3 %copy-start.26 = (s32[1,1024]{1,0:T(1,128)}, s32[1,1024]{1,0:T(1,128)S(1)}, u32[]{:S(2)}) copy-start(s32[1,1024]{1,0:T(1,128)S(1)} %get-tuple-element.56) | copy-start | bytes 12292
  11.1 125.3 %copy-start.31 = (pred[1024]{0:T(1024)(128)(4,1)}, pred[1024]{0:T(1024)(128)(4,1)S(1)}, u32[]{:S(2)}) copy-start(pred[1024]{0:T(1024)(128)(4,1)S(1)} %get-tuple-element.34) | copy-start | bytes 3076
  11.1 125.3 %copy-start.33 = (pred[1024]{0:T(1024)(128)(4,1)}, pred[1024]{0:T(1024)(128)(4,1)S(1)}, u32[]{:S(2)}) copy-start(pred[1024]{0:T(1024)(128)(4,1)S(1)} %get-tuple-element.55) | copy-start | bytes 3076
  136.5 26.3 %copy-start.3 = (f32[1024,512]{1,0:T(8,128)}, f32[1024,512]{1,0:T(8,128)S(1)}, u32[]{:S(2)}) copy-start(f32[1024,512]{1,0:T(8,128)S(1)} %get-tuple-element.51) | copy-start | bytes 6291460
  162.8 92.1 %all-gather.5.cloned.1.call-start = ((), (), s32[]{:S(2)}) async-start(), calls=%async_computation.7 | async-start | bytes 5242880 | tf_op jit(solution)/shard_map/all_gather | solution.py:53
  223.9 92.5 %all-reduce.8.cloned.1.call-start = ((), (), s32[]{:S(2)}) async-start(), calls=%async_computation.8 | async-start | bytes 262144 | tf_op jit(solution)/shard_map/psum | solution.py:61
  261.4 25.7 %copy-start.11 = (bf16[512,64]{0,1:T(8,128)(2,1)S(1)}, bf16[512,64]{0,1:T(8,128)(2,1)}, u32[]{:S(2)}) copy-start(bf16[512,64]{0,1:T(8,128)(2,1)} %param.20) | copy-start | bytes 196612
  282.9 33.6 %copy-start.9 = (f32[1024,64]{0,1:T(8,128)S(1)}, f32[1024,64]{0,1:T(8,128)}, u32[]{:S(2)}) copy-start(f32[1024,64]{0,1:T(8,128)} %param.23) | copy-start | bytes 786436
  286.1 1.0 copy-start.1
  288.2 104.2 %reduce-scatter.7.cloned.1.call-start = ((), (), s32[]{:S(2)}) async-start(), calls=%async_computation.9 | async-start | bytes 5242880 | tf_op jit(solution)/shard_map/reduce_scatter | solution.py:104
  343.3 3.0 copy-start.12
  343.3 3.0 copy-start.16
  343.3 4.0 copy-start.35
  346.3 1.0 copy-start.5
  351.6 115.8 %reduce-scatter.9.cloned.1.call-start = ((), (), s32[]{:S(2)}) async-start(), calls=%async_computation.10 | async-start | bytes 5242880 | tf_op jit(solution)/shard_map/reduce_scatter | solution.py:104
  418.8 2.4 copy-start.14
  418.8 2.4 copy-start.18
  418.8 3.4 copy-start.36
  421.1 1.0 copy-start.7
  426.5 1.2 copy-start.2
  426.5 1.2 copy-start.10
  426.5 2.4 copy-start.6
  426.5 194.7 %reduce-scatter.17.cloned.1.call-start = ((), (), s32[]{:S(2)}) async-start(), calls=%async_computation.14 | async-start | bytes 147456 | tf_op jit(solution)/shard_map/reduce_scatter | solution.py:63
  428.9 193.7 %reduce-scatter.15.cloned.1.call-start = ((), (), s32[]{:S(2)}) async-start(), calls=%async_computation.13 | async-start | bytes 2359296 | tf_op jit(solution)/shard_map/reduce_scatter | solution.py:95
  435.3 1.2 copy-start.8
  435.3 239.3 %reduce-scatter.13.cloned.1.call-start = ((), (), s32[]{:S(2)}) async-start(), calls=%async_computation.12 | async-start | bytes 2359296 | tf_op jit(solution)/shard_map/reduce_scatter | solution.py:95
  442.4 25.0 %copy-start.4 = (f32[1024,512]{1,0:T(8,128)S(1)}, f32[1024,512]{1,0:T(8,128)}, u32[]{:S(2)}) copy-start(f32[1024,512]{1,0:T(8,128)} %copy-done.3) | copy-start | bytes 6291460
  442.4 51.8 %copy-start.21 = (s32[1024]{0:T(1024)S(1)}, s32[1024]{0:T(1024)}, u32[]{:S(2)}) copy-start(s32[1024]{0:T(1024)} %copy-done.20) | copy-start | bytes 12292
  442.4 51.8 %copy-start.23 = (f32[1024]{0:T(1024)S(1)}, f32[1024]{0:T(1024)}, u32[]{:S(2)}) copy-start(f32[1024]{0:T(1024)} %copy-done.22) | copy-start | bytes 12292
  442.4 51.8 %copy-start.25 = (s32[1,1024]{1,0:T(1,128)S(1)}, s32[1,1024]{1,0:T(1,128)}, u32[]{:S(2)}) copy-start(s32[1,1024]{1,0:T(1,128)} %copy-done.24) | copy-start | bytes 12292
  442.4 51.8 %copy-start.27 = (s32[1,1024]{1,0:T(1,128)S(1)}, s32[1,1024]{1,0:T(1,128)}, u32[]{:S(2)}) copy-start(s32[1,1024]{1,0:T(1,128)} %copy-done.26) | copy-start | bytes 12292
  442.4 51.8 %copy-start.28 = (f32[512]{0:T(512)S(1)}, f32[512]{0:T(512)}, u32[]{:S(2)}) copy-start(f32[512]{0:T(512)} %get-tuple-element.42) | copy-start | bytes 6148
  442.5 51.8 %copy-start.30 = (pred[1024]{0:T(1024)(128)(4,1)S(1)}, pred[1024]{0:T(1024)(128)(4,1)}, u32[]{:S(2)}) copy-start(pred[1024]{0:T(1024)(128)(4,1)} %copy-done.29) | copy-start | bytes 3076
  442.5 51.8 %copy-start.32 = (pred[1024]{0:T(1024)(128)(4,1)S(1)}, pred[1024]{0:T(1024)(128)(4,1)}, u32[]{:S(2)}) copy-start(pred[1024]{0:T(1024)(128)(4,1)} %copy-done.31) | copy-start | bytes 3076
  442.5 51.8 %copy-start.34 = (pred[1024]{0:T(1024)(128)(4,1)S(1)}, pred[1024]{0:T(1024)(128)(4,1)}, u32[]{:S(2)}) copy-start(pred[1024]{0:T(1024)(128)(4,1)} %copy-done.33) | copy-start | bytes 3076
  442.5 51.8 %copy-start.37 = (s32[1024]{0:T(1024)S(1)}, s32[1024]{0:T(1024)}, u32[]{:S(2)}) copy-start(s32[1024]{0:T(1024)} %param.15) | copy-start | bytes 12292
  442.5 51.8 %copy-start.38 = (s32[1024]{0:T(1024)S(1)}, s32[1024]{0:T(1024)}, u32[]{:S(2)}) copy-start(s32[1024]{0:T(1024)} %param.13) | copy-start | bytes 12292
  442.5 51.8 %copy-start.39 = (s32[1024]{0:T(1024)S(1)}, s32[1024]{0:T(1024)}, u32[]{:S(2)}) copy-start(s32[1024]{0:T(1024)} %param.14) | copy-start | bytes 12292
  442.5 298.6 %reduce-scatter.11.cloned.1.call-start = ((), (), s32[]{:S(2)}) async-start(), calls=%async_computation.11 | async-start | bytes 1179648 | tf_op jit(solution)/shard_map/reduce_scatter | solution.py:87
  621.2 55.5 %copy-start.17 = (f32[512]{0:T(512)S(1)}, f32[512]{0:T(512)}, u32[]{:S(2)}) copy-start(f32[512]{0:T(512)} %copy-done.16) | copy-start | bytes 6148
  621.2 55.5 %copy-start.19 = (f32[512]{0:T(512)S(1)}, f32[512]{0:T(512)}, u32[]{:S(2)}) copy-start(f32[512]{0:T(512)} %copy-done.18) | copy-start | bytes 6148
  621.2 56.1 %copy-start.13 = (f32[512]{0:T(512)S(1)}, f32[512]{0:T(512)}, u32[]{:S(2)}) copy-start(f32[512]{0:T(512)} %copy-done.12) | copy-start | bytes 6148
  621.2 56.1 %copy-start.15 = (f32[512]{0:T(512)S(1)}, f32[512]{0:T(512)}, u32[]{:S(2)}) copy-start(f32[512]{0:T(512)} %copy-done.14) | copy-start | bytes 6148
Sparse Core Ops, SparseCore 0:
  162.9 31.6 all-gather.2
  224.1 30.7 all-gather.4
  288.3 28.0 all-reduce.7
  351.7 40.6 reduce-scatter.6
  426.6 40.7 reduce-scatter.8
  471.2 61.8 reduce-scatter.16
  536.5 67.3 reduce-scatter.14
  607.4 67.1 reduce-scatter.12
  678.0 63.1 reduce-scatter.10
where the time goes:
time: 759 us; the launch traced here: 750 us
  matrix products  292 us (38%)
  waiting for transfers between devices  272 us (36%)
  blocking collectives  131 us (17%)
  other arithmetic  32.5 us (4%)
  between operations  14.5 us (2%)
    dot_general x4, matrix products, column_products(): return jnp.dot(left_rows.T, right_rows, preferred_element_type=jnp.float32)  140 us
    dot_general x1, matrix products, per_device(): summed = jnp.dot(whole_input, w_in, preferred_element_type=jnp.float32)  125 us
    reduce_scatter x3, waiting for transfers between devices, per_device(): lax.psum_scatter(column_products(whole_input, slope_z).astype(jnp.bfloat1...  115 us
    psum x3, blocking collectives, column_stats(): lax.psum((jnp.sum(summed, axis=0), jnp.sum(summed * summed, axis=0)), 'dp')  66.2 us
    reduce_scatter x2, waiting for transfers between devices, per_device(): lax.psum_scatter(partial_in.astype(jnp.bfloat16), 'mp', scatter_dimension...  65.4 us
    psum x3, blocking collectives, per_device(): lax.psum((jnp.sum(slope_a, axis=0), jnp.sum(slope_a * normed, axis=0)), '...  64.5 us
    all_gather x2, waiting for transfers between devices, per_device(): whole_input = lax.all_gather(current, 'mp', axis=1, tiled=True)  62.7 us
    psum x1, waiting for transfers between devices, per_device(): lax.psum(partial_out.astype(jnp.bfloat16), 'mp').astype(jnp.float32)  28.2 us
  transfers between devices with their start and end apart: 9, of which 7 were waited for; matrix products, arithmetic and copies ran while one was open for 20% of the time, Pallas kernels for 0%

commit v1 on v0

--- a/solution.py
+++ b/solution.py
@@ -1,18 +1,86 @@
+import functools
 import math
 
 import jax
 import jax.numpy as jnp
 from jax import lax
+from jax.experimental import pallas as pl
+from jax.experimental.pallas import tpu as pltpu
 from jax.sharding import PartitionSpec as P
 
 epsilon_norm = 1e-05
 
 
 def encode(ids, hash_a, hash_b, hash_p, hash_m):
-    reduced = ids[:, None] % hash_p[None, :]
-    hashed = (hash_a[None, :] * reduced + hash_b[None, :]) % hash_p[None, :] % hash_m[None, :]
-    scaled = 2.0 * hashed.astype(jnp.float32) / (hash_m[None, :] - 1).astype(jnp.float32) - 1.0
-    return scaled.astype(jnp.bfloat16)
+    p_real = hash_p.astype(jnp.float32)
+    m_real = hash_m.astype(jnp.float32)
+    p_inv, m_inv, scale = lax.optimization_barrier(
+        (1.0 / p_real, 1.0 / m_real, 2.0 / (hash_m - 1).astype(jnp.float32))
+    )
+    ids_real = ids.astype(jnp.float32)
+    guess = (ids_real[:, None] * p_inv[None, :]).astype(jnp.int32)
+    reduced = ids[:, None] - guess * hash_p[None, :]
+    mixed = hash_a[None, :] * reduced + hash_b[None, :]
+    guess = jnp.floor(mixed.astype(jnp.float32) * p_inv[None, :]).astype(jnp.int32)
+    rest = (mixed - guess * hash_p[None, :]).astype(jnp.float32)
+    rest = jnp.where(rest < 0.0, rest + p_real[None, :], rest)
+    rest = jnp.where(rest >= p_real[None, :], rest - p_real[None, :], rest)
+    bucket = jnp.floor((rest + 0.5) * m_inv[None, :])
+    hashed = rest - bucket * m_real[None, :]
+    return (hashed * scale[None, :] - 1.0).astype(jnp.bfloat16)
+
+
+def exchange_kernel(axis, n, x_ref, o_ref, held, send_sems, recv_sems):
+    me = lax.axis_index(axis)
+    barrier = pltpu.get_barrier_semaphore()
+    for step in range(1, n):
+        pl.semaphore_signal(
+            barrier,
+            inc=1,
+            device_id={axis: lax.rem(me + step, n)},
+            device_id_type=pl.DeviceIdType.MESH,
+        )
+    pl.semaphore_wait(barrier, n - 1)
+    copies = []
+    for step in range(1, n):
+        copy = pltpu.make_async_remote_copy(
+            src_ref=x_ref,
+            dst_ref=held.at[me],
+            send_sem=send_sems.at[step],
+            recv_sem=recv_sems.at[step],
+            device_id={axis: lax.rem(me + step, n)},
+            device_id_type=pl.DeviceIdType.MESH,
+        )
+        copy.start()
+        copies.append(copy)
+    held[me] = x_ref[...]
+    for copy in copies:
+        copy.wait()
+    total = held[0]
+    for at in range(1, n):
+        total = total + held[at]
+    o_ref[...] = total
+
+
+def sum_pair(first, second, axis):
+    n = lax.axis_size(axis)
+    stacked = jnp.stack([first, second]).reshape(8, -1)
+    total = pl.pallas_call(
+        functools.partial(exchange_kernel, axis, n),
+        out_shape=jax.ShapeDtypeStruct(stacked.shape, stacked.dtype),
+        in_specs=[pl.BlockSpec(memory_space=pltpu.VMEM)],
+        out_specs=pl.BlockSpec(memory_space=pltpu.VMEM),
+        scratch_shapes=[
+            pltpu.VMEM((n,) + stacked.shape, stacked.dtype),
+            pltpu.SemaphoreType.DMA((n,)),
+            pltpu.SemaphoreType.DMA((n,)),
+        ],
+        compiler_params=pltpu.CompilerParams(
+            collective_id=0, has_side_effects=True, vmem_limit_bytes=4 << 20
+        ),
+        name="sum_pair",
+    )(stacked).reshape(2, -1)
+    return total[0], total[1]
 
 
 def mish_act(values):
@@ -25,7 +93,7 @@
 
 
 def column_stats(summed, batch_total):
-    totals, squares = lax.psum((jnp.sum(summed, axis=0), jnp.sum(summed * summed, axis=0)), "dp")
+    totals, squares = sum_pair(jnp.sum(summed, axis=0), jnp.sum(summed * summed, axis=0), "dp")
     average = totals / batch_total
     spread = squares / batch_total - average * average
     centered = summed - average
@@ -41,7 +109,7 @@
     batch_devices = lax.axis_size("dp")
     batch_total = ids.shape[0] * batch_devices
     layer_count = bn_gain.shape[0]
-    encoded = encode(ids, hash_a, hash_b, hash_p, hash_m)
+    encoded = lax.optimization_barrier(encode(ids, hash_a, hash_b, hash_p, hash_m))
     full_inputs = []
     saved = []
     current = encoded
@@ -74,8 +142,8 @@
     for layer_at in reversed(range(layer_count)):
         normed, inverse, shifted = saved[layer_at]
         slope_a = upstream * mish_slope(shifted)
-        bias_sum, gain_sum = lax.psum(
-            (jnp.sum(slope_a, axis=0), jnp.sum(slope_a * normed, axis=0)), "dp"
+        bias_sum, gain_sum = sum_pair(
+            jnp.sum(slope_a, axis=0), jnp.sum(slope_a * normed, axis=0), "dp"
         )
         slope_z = (
             bn_gain[layer_at]

time: 759 us -> 578 us (0.76); the launches traced: 750 us -> 577 us
  matrix products: 292 us -> 46 us
  waiting for transfers between devices: 272 us -> 428 us
  blocking collectives: 131 us -> 0 us
  Pallas kernels: 0 us -> 42.4 us
    psum x6 -> x0, blocking collectives: 131 us -> none  [the longest x3 66.2 us: column_stats(): lax.psum((jnp.sum(summed, axis=0), jnp.sum(summed * summed, axis=0)), 'dp')]
    dot_general x1, matrix products: 125 us -> 1.28 us  [per_device(): summed = jnp.dot(whole_input, w_in, preferred_element_type=jnp.float32)]
    dot_general x4, matrix products: 140 us -> 17.7 us  [column_products(): return jnp.dot(left_rows.T, right_rows, preferred_element_type=jnp.float32)]
    reduce_scatter x3, waiting for transfers between devices: 115 us -> 204 us  [per_device(): lax.psum_scatter(column_products(whole_input, slope_z).astype(jnp.bfloat1...]
    reduce_scatter x1, waiting for transfers between devices: 0.02 us -> 49.2 us  [per_device(): lax.psum_scatter(column_products(current, residual_out).astype(jnp.bfloat...]
    pallas_call x0 -> x6, Pallas kernels: none -> 42.4 us  [sum_pair(): pl.pallas_call(functools.partial(exchange_kernel, axis, n), out_shape=jax...]
  transfers between devices with their start and end apart: 9 -> 9, of which waited for: 7 -> 9; matrix products, arithmetic and copies ran while one was open for 20% -> 5% of each run, Pallas kernels for 0% -> 1%
where the time goes in v1:
time: 578 us; the launch traced here: 577 us
  waiting for transfers between devices  428 us (74%)
  matrix products  46 us (8%)
  Pallas kernels  42.4 us (7%)
  other arithmetic  39.8 us (7%)
  between operations  14.2 us (2%)
  local copies, waits for them, and re-layouts  6.21 us (1%)
    reduce_scatter x3, waiting for transfers between devices, per_device(): lax.psum_scatter(column_products(whole_input, slope_z).astype(jnp.bfloat1...  204 us
    reduce_scatter x2, waiting for transfers between devices, per_device(): lax.psum_scatter(partial_in.astype(jnp.bfloat16), 'mp', scatter_dimension...  72.7 us
    all_gather x2, waiting for transfers between devices, per_device(): whole_input = lax.all_gather(current, 'mp', axis=1, tiled=True)  69.9 us
    reduce_scatter x1, waiting for transfers between devices, per_device(): lax.psum_scatter(column_products(current, residual_out).astype(jnp.bfloat...  49.2 us
    pallas_call x6, Pallas kernels, sum_pair(): pl.pallas_call(functools.partial(exchange_kernel, axis, n), out_shape=jax...  42.4 us
    psum x1, waiting for transfers between devices, per_device(): lax.psum(partial_out.astype(jnp.bfloat16), 'mp').astype(jnp.float32)  31.6 us
    dot_general x4, matrix products, column_products(): return jnp.dot(left_rows.T, right_rows, preferred_element_type=jnp.float32)  17.7 us
    dot_general x2, matrix products, per_device(): jnp.dot(whole_input, w_mid[layer_at - 1], preferred_element_type=jnp.floa...  11.8 us
  transfers between devices with their start and end apart: 9, of which 9 were waited for; matrix products, arithmetic and copies ran while one was open for 5% of the time, Pallas kernels for 1%

profile of v1, /device:TPU:0, one launch (start us, length us, event | category | flops | bytes accessed | tf_op | source)
XLA Modules:
  0.0 577.0 jit_solution(10947299816164392302)
XLA Ops:
  7.2 0.0 all-gather.3.cloned.1.call-start
  7.2 0.8 convert_element_type.88
  8.0 0.7 convert_element_type.87
  8.7 0.8 convert_divide_fusion
  9.5 0.7 convert_element_type.86
  10.1 5.4 add_convert_fusion
  15.6 1.3 fusion.40
  16.9 8.6 %sum_pair.6 = f32[8,128]{1,0:T(8,128)S(1)} custom-call(f32[8,128]{1,0:T(8,128)S(1)} %reshape.242.x_ref), custom_call_target="tpu_custom_call" | custom-call | tf_op jit(solution)/shard_map/sum_pair/pallas_call | solution.py:68
  25.6 0.6 copy-done.13
  26.2 2.5 fusion.10
  28.7 0.0 all-gather.3.cloned.1.call-update
  28.7 0.0 all-gather.5.cloned.1.call-start
  28.8 35.4 %all-gather.3.cloned.1.call-done = bf16[1024,2048]{1,0:T(8,128)(2,1)} async-done(((bf16[1024,512]{1,0:T(8,128)(2,1)}), bf16[1024,2048]{1,0:T(8,128)(2,1)}) %all-gather.3.cloned.1.call-update) | async-done | bytes 4194320 | tf_op jit(solution)/shard_map/all_gather | solution.py:121
  64.1 5.2 fusion.39
  69.4 6.8 %sum_pair.7 = f32[8,128]{1,0:T(8,128)S(1)} custom-call(f32[8,128]{1,0:T(8,128)S(1)} %reshape.243.x_ref), custom_call_target="tpu_custom_call" | custom-call | tf_op jit(solution)/shard_map/sum_pair/pallas_call | solution.py:68
  76.2 2.5 fusion.12
  78.7 0.0 all-reduce.2.cloned.1.call-start
  78.8 34.5 %all-gather.5.cloned.1.call-done = bf16[1024,2048]{1,0:T(8,128)(2,1)} async-done(((bf16[1024,512]{1,0:T(8,128)(2,1)}), bf16[1024,2048]{1,0:T(8,128)(2,1)}) %all-gather.5.cloned.1.call-update) | async-done | bytes 4194320 | tf_op jit(solution)/shard_map/all_gather | solution.py:121
  113.3 6.6 %fusion.38 = (f32[512]{0:T(512)S(1)}, f32[512]{0:T(512)S(1)}, f32[1024,512]{1,0:T(8,128)}) fusion(bf16[1024,2048]{1,0:T(8,128)(2,1)} %all-gather.5.cloned.1.call-done, bf16[2,2048,512]{2,1,0:T(8,128)(2,1)} %param.17), kind=kOutput, calls=%fused_computation.106 | convolution fusion | flops 2149055488 | bytes 8392704 | tf_op jit(solution)/shard_map/dot_general | solution.py:122
  119.8 6.8 %sum_pair.8 = f32[8,128]{1,0:T(8,128)S(1)} custom-call(f32[8,128]{1,0:T(8,128)S(1)} %reshape.244.x_ref), custom_call_target="tpu_custom_call" | custom-call | tf_op jit(solution)/shard_map/sum_pair/pallas_call | solution.py:68
  126.6 0.6 slice_multiply_fusion.8
  127.2 3.2 fusion.14
  130.4 1.0 copy-done.1
  131.4 1.1 convolution_convert_fusion.5
  132.5 0.0 all-reduce.2.cloned.1.call-update
  132.5 0.2 reduce-scatter.7.cloned.1.call-start
  132.7 31.6 %all-reduce.2.cloned.1.call-done = bf16[1024,64]{0,1:T(8,128)(2,1)} async-done(((bf16[1024,64]{0,1:T(8,128)(2,1)}), bf16[1024,64]{0,1:T(8,128)(2,1)}) %all-reduce.2.cloned.1.call-update) | async-done | bytes 131088 | tf_op jit(solution)/shard_map/psum | solution.py:129
  164.3 5.5 fusion.37
  169.8 6.8 %sum_pair.9 = f32[8,128]{1,0:T(8,128)S(1)} custom-call(f32[8,128]{1,0:T(8,128)S(1)} %reshape.245.x_ref), custom_call_target="tpu_custom_call" | custom-call | tf_op jit(solution)/shard_map/sum_pair/pallas_call | solution.py:68
  176.6 0.6 fusion.45
  177.2 3.0 multiply_convert_fusion.2
  180.2 1.0 copy-done.6
  181.1 4.3 convolution_convert_fusion.1
  185.5 0.0 reduce-scatter.9.cloned.1.call-start
  185.6 44.4 %reduce-scatter.7.cloned.1.call-done = bf16[1024,512]{1,0:T(8,128)(2,1)} async-done(((bf16[1024,2048]{1,0:T(8,128)(2,1)}), bf16[1024,512]{1,0:T(8,128)(2,1)}) %reduce-scatter.7.cloned.1.call-update) | async-done | bytes 1048592 | tf_op jit(solution)/shard_map/reduce_scatter | solution.py:172
  230.0 5.0 fusion.36
  235.0 6.8 %sum_pair.10 = f32[8,128]{1,0:T(8,128)S(1)} custom-call(f32[8,128]{1,0:T(8,128)S(1)} %reshape.246.x_ref), custom_call_target="tpu_custom_call" | custom-call | tf_op jit(solution)/shard_map/sum_pair/pallas_call | solution.py:68
  241.7 0.6 fusion.44
  242.4 2.3 multiply_convert_fusion.1
  244.7 1.0 copy-done.8
  245.7 4.3 convolution_convert_fusion
  250.1 0.0 reduce-scatter.17.cloned.1.call-start
  250.1 1.1 copy-done.2
  251.3 1.1 convolution_convert_fusion.6
  252.4 0.3 reduce-scatter.15.cloned.1.call-start
  252.7 5.9 %convolution_convert_fusion.2 = bf16[2048,512]{1,0:T(8,128)(2,1)} fusion(bf16[1024,2048]{1,0:T(8,128)(2,1)} %all-gather.5.cloned.1.call-done, bf16[1024,512]{1,0:T(8,128)(2,1)S(1)} %copy-done.7), kind=kOutput, calls=%fused_computation.8 | convolution fusion | flops 2148532224 | bytes 7340032 | tf_op jit(solution)/shard_map/dot_general | solution.py:105
  258.6 0.0 reduce-scatter.13.cloned.1.call-start
  258.7 1.4 copy-done.9
  260.1 6.1 %convolution_convert_fusion.3 = bf16[2048,512]{1,0:T(8,128)(2,1)} fusion(bf16[1024,2048]{1,0:T(8,128)(2,1)} %all-gather.3.cloned.1.call-done, bf16[1024,512]{1,0:T(8,128)(2,1)S(1)} %copy-done.9), kind=kOutput, calls=%fused_computation.9 | convolution fusion | flops 2148532224 | bytes 7340032 | tf_op jit(solution)/shard_map/dot_general | solution.py:105
  266.2 0.0 reduce-scatter.11.cloned.1.call-start
  266.2 28.3 %reduce-scatter.9.cloned.1.call-done = bf16[1024,512]{1,0:T(8,128)(2,1)} async-done(((bf16[1024,2048]{1,0:T(8,128)(2,1)}), bf16[1024,512]{1,0:T(8,128)(2,1)}) %reduce-scatter.9.cloned.1.call-update) | async-done | bytes 1048592 | tf_op jit(solution)/shard_map/reduce_scatter | solution.py:172
  294.5 4.9 fusion.35
  299.5 6.8 %sum_pair.11 = f32[8,128]{1,0:T(8,128)S(1)} custom-call(f32[8,128]{1,0:T(8,128)S(1)} %reshape.247.x_ref), custom_call_target="tpu_custom_call" | custom-call | tf_op jit(solution)/shard_map/sum_pair/pallas_call | solution.py:68
  306.3 4.6 convolution_convert_fusion.4
  310.9 0.0 reduce-scatter.11.cloned.1.call-update
  310.9 49.2 %reduce-scatter.17.cloned.1.call-done = bf16[64,64]{1,0:T(8,128)(2,1)} async-done(((bf16[512,64]{1,0:T(8,128)(2,1)}), bf16[64,64]{1,0:T(8,128)(2,1)}) %reduce-scatter.17.cloned.1.call-update) | async-done | bytes 8208 | tf_op jit(solution)/shard_map/reduce_scatter | solution.py:131
  360.1 1.3 convert_element_type.113
  361.5 69.7 %reduce-scatter.15.cloned.1.call-done = bf16[256,512]{1,0:T(8,128)(2,1)} async-done(((bf16[2048,512]{1,0:T(8,128)(2,1)}), bf16[256,512]{1,0:T(8,128)(2,1)}) %reduce-scatter.15.cloned.1.call-update) | async-done | bytes 262160 | tf_op jit(solution)/shard_map/reduce_scatter | solution.py:163
  431.1 71.0 %reduce-scatter.13.cloned.1.call-done = bf16[256,512]{1,0:T(8,128)(2,1)} async-done(((bf16[2048,512]{1,0:T(8,128)(2,1)}), bf16[256,512]{1,0:T(8,128)(2,1)}) %reduce-scatter.13.cloned.1.call-update) | async-done | bytes 262160 | tf_op jit(solution)/shard_map/reduce_scatter | solution.py:163
  502.1 2.1 maximum_convert_fusion
  504.2 0.6 pad_maximum_fusion.1
  504.8 0.6 pad_maximum_fusion
  505.4 63.4 %reduce-scatter.11.cloned.1.call-done = bf16[128,512]{1,0:T(8,128)(2,1)} async-done(((bf16[1024,512]{1,0:T(8,128)(2,1)}), bf16[128,512]{1,0:T(8,128)(2,1)}) %reduce-scatter.11.cloned.1.call-update) | async-done | bytes 131088 | tf_op jit(solution)/shard_map/reduce_scatter | solution.py:155
  568.8 1.6 convert_element_type.109
  (69 shorter events, 0.4 us)
Async XLA Ops:
  7.2 8.4 %copy-start = (bf16[1024,512]{1,0:T(8,128)(2,1)S(1)}, bf16[1024,512]{1,0:T(8,128)(2,1)}, u32[]{:S(2)}) copy-start(bf16[1024,512]{1,0:T(8,128)(2,1)} %param.16) | copy-start | bytes 3145732
  7.2 57.0 %all-gather.3.cloned.1.call-start = ((), (), s32[]{:S(2)}) async-start(), calls=%async_computation.6 | async-start | bytes 5242880 | tf_op jit(solution)/shard_map/all_gather | solution.py:121
  15.6 1.3 copy-start.5
  15.6 10.0 %copy-start.15 = (f32[3,512]{1,0:T(4,128)S(1)}, f32[3,512]{1,0:T(4,128)}, u32[]{:S(2)}) copy-start(f32[3,512]{1,0:T(4,128)} %param.19) | copy-start | bytes 18436
  15.6 10.0 %copy-start.20 = (f32[3,512]{1,0:T(4,128)S(1)}, f32[3,512]{1,0:T(4,128)}, u32[]{:S(2)}) copy-start(f32[3,512]{1,0:T(4,128)} %param.20) | copy-start | bytes 18436
  16.9 11.8 %copy-start.3 = (f32[1024,512]{1,0:T(8,128)}, f32[1024,512]{1,0:T(8,128)S(1)}, u32[]{:S(2)}) copy-start(f32[1024,512]{1,0:T(8,128)S(1)} %get-tuple-element.54) | copy-start | bytes 6291460
  25.6 0.6 copy-start.13
  28.7 84.6 %all-gather.5.cloned.1.call-start = ((), (), s32[]{:S(2)}) async-start(), calls=%async_computation.7 | async-start | bytes 5242880 | tf_op jit(solution)/shard_map/all_gather | solution.py:121
  78.7 85.6 %all-reduce.2.cloned.1.call-start = ((), (), s32[]{:S(2)}) async-start(), calls=%async_computation.8 | async-start | bytes 262144 | tf_op jit(solution)/shard_map/psum | solution.py:129
  119.8 11.6 %copy-start.12 = (bf16[512,64]{0,1:T(8,128)(2,1)S(1)}, bf16[512,64]{0,1:T(8,128)(2,1)}, u32[]{:S(2)}) copy-start(bf16[512,64]{0,1:T(8,128)(2,1)} %param.18) | copy-start | bytes 196612
  127.2 37.1 %copy-start.10 = (f32[1024,64]{0,1:T(8,128)S(1)}, f32[1024,64]{0,1:T(8,128)}, u32[]{:S(2)}) copy-start(f32[1024,64]{0,1:T(8,128)} %param.21) | copy-start | bytes 786436
  130.4 1.0 copy-start.1
  132.5 97.5 %reduce-scatter.7.cloned.1.call-start = ((), (), s32[]{:S(2)}) async-start(), calls=%async_computation.9 | async-start | bytes 5242880 | tf_op jit(solution)/shard_map/reduce_scatter | solution.py:172
  177.2 3.9 copy-start.22
  180.2 1.0 copy-start.6
  185.5 109.0 %reduce-scatter.9.cloned.1.call-start = ((), (), s32[]{:S(2)}) async-start(), calls=%async_computation.10 | async-start | bytes 5242880 | tf_op jit(solution)/shard_map/reduce_scatter | solution.py:172
  242.3 3.3 copy-start.23
  244.7 1.0 copy-start.8
  250.0 1.2 copy-start.2
  250.0 1.2 copy-start.11
  250.0 2.7 copy-start.7
  250.1 110.1 %reduce-scatter.17.cloned.1.call-start = ((), (), s32[]{:S(2)}) async-start(), calls=%async_computation.14 | async-start | bytes 147456 | tf_op jit(solution)/shard_map/reduce_scatter | solution.py:131
  252.4 178.7 %reduce-scatter.15.cloned.1.call-start = ((), (), s32[]{:S(2)}) async-start(), calls=%async_computation.13 | async-start | bytes 2359296 | tf_op jit(solution)/shard_map/reduce_scatter | solution.py:163
  258.6 1.5 copy-start.9
  258.6 243.5 %reduce-scatter.13.cloned.1.call-start = ((), (), s32[]{:S(2)}) async-start(), calls=%async_computation.12 | async-start | bytes 2359296 | tf_op jit(solution)/shard_map/reduce_scatter | solution.py:163
  266.1 28.4 %copy-start.4 = (f32[1024,512]{1,0:T(8,128)S(1)}, f32[1024,512]{1,0:T(8,128)}, u32[]{:S(2)}) copy-start(f32[1024,512]{1,0:T(8,128)} %copy-done.3) | copy-start | bytes 6291460
  266.2 28.4 %copy-start.14 = (f32[1,512]{1,0:T(1,128)S(1)}, f32[1,512]{1,0:T(1,128)}, u32[]{:S(2)}) copy-start(f32[1,512]{1,0:T(1,128)} %copy-done.13) | copy-start | bytes 6148
  266.2 40.1 %copy-start.21 = (f32[1,512]{1,0:T(1,128)S(1)}, f32[1,512]{1,0:T(1,128)}, u32[]{:S(2)}) copy-start(f32[1,512]{1,0:T(1,128)} %get-tuple-element.25) | copy-start | bytes 6148
  266.2 302.6 %reduce-scatter.11.cloned.1.call-start = ((), (), s32[]{:S(2)}) async-start(), calls=%async_computation.11 | async-start | bytes 1179648 | tf_op jit(solution)/shard_map/reduce_scatter | solution.py:155
  310.9 193.3 %copy-start.17 = (f32[4,128]{1,0:T(4,128)S(1)}, f32[4,128]{1,0:T(4,128)}, u32[]{:S(2)}) copy-start(f32[4,128]{1,0:T(4,128)} %get-tuple-element.42) | copy-start | bytes 6148
  310.9 193.3 %copy-start.19 = (f32[4,128]{1,0:T(4,128)S(1)}, f32[4,128]{1,0:T(4,128)}, u32[]{:S(2)}) copy-start(f32[4,128]{1,0:T(4,128)} %get-tuple-element.38) | copy-start | bytes 6148
  310.9 193.9 %copy-start.16 = (f32[4,128]{1,0:T(4,128)S(1)}, f32[4,128]{1,0:T(4,128)}, u32[]{:S(2)}) copy-start(f32[4,128]{1,0:T(4,128)} %get-tuple-element.45) | copy-start | bytes 6148
  310.9 193.9 %copy-start.18 = (f32[4,128]{1,0:T(4,128)S(1)}, f32[4,128]{1,0:T(4,128)}, u32[]{:S(2)}) copy-start(f32[4,128]{1,0:T(4,128)} %get-tuple-element.41) | copy-start | bytes 6148
Sparse Core Ops, SparseCore 0:
  28.8 35.2 all-gather.2
  78.8 34.3 all-gather.4
  132.6 31.6 all-reduce.1
  185.6 44.3 reduce-scatter.6
  250.2 44.3 reduce-scatter.8
  298.3 61.8 reduce-scatter.16
  363.7 67.4 reduce-scatter.14
  434.7 67.3 reduce-scatter.12
  505.5 63.2 reduce-scatter.10

commit v2 on v1

--- a/solution.py
+++ b/solution.py
@@ -56,31 +56,261 @@
     held[me] = x_ref[...]
     for copy in copies:
         copy.wait()
-    total = held[0]
+    total = held[0].astype(jnp.float32)
     for at in range(1, n):
-        total = total + held[at]
+        total = total + held[at].astype(jnp.float32)
     o_ref[...] = total
 
 
-def sum_pair(first, second, axis):
+def exchange_sum(value, axis, collective, name):
     n = lax.axis_size(axis)
-    stacked = jnp.stack([first, second]).reshape(8, -1)
-    total = pl.pallas_call(
+    return pl.pallas_call(
         functools.partial(exchange_kernel, axis, n),
-        out_shape=jax.ShapeDtypeStruct(stacked.shape, stacked.dtype),
-        in_specs=[pl.BlockSpec(memory_space=pltpu.VMEM)],
-        out_specs=pl.BlockSpec(memory_space=pltpu.VMEM),
+        out_shape=jax.ShapeDtypeStruct(value.shape, jnp.float32),
+        in_specs=[VMEM_SPEC],
+        out_specs=VMEM_SPEC,
         scratch_shapes=[
-            pltpu.VMEM((n,) + stacked.shape, stacked.dtype),
+            pltpu.VMEM((n,) + value.shape, value.dtype),
             pltpu.SemaphoreType.DMA((n,)),
             pltpu.SemaphoreType.DMA((n,)),
         ],
         compiler_params=pltpu.CompilerParams(
-            collective_id=0, has_side_effects=True, vmem_limit_bytes=4 << 20
+            collective_id=collective, has_side_effects=True, vmem_limit_bytes=4 << 20
         ),
-        name="sum_pair",
-    )(stacked).reshape(2, -1)
+        name=name,
+    )(value)
+
+
+def sum_pair(first, second, axis):
+    total = exchange_sum(jnp.stack([first, second]).reshape(8, -1), axis, 0, "sum_pair")
+    total = total.reshape(2, -1)
     return total[0], total[1]
+
+
+VMEM_SPEC = pl.BlockSpec(memory_space=pltpu.VMEM)
+MESH_ID = pl.DeviceIdType.MESH
+CHUNKS = 4
+
+
+def meet(targets):
+    barrier = pltpu.get_barrier_semaphore()
+    for target in targets:
+        pl.semaphore_signal(barrier, inc=1, device_id=target, device_id_type=MESH_ID)
+    pl.semaphore_wait(barrier, len(targets))
+
+
+def quad_peers(axis):
+    me = lax.axis_index(axis)
+    near = me + 1 - 2 * lax.rem(me, 2)
+    far = lax.rem(me + 2, 4)
+    return me, near, far
+
+
+def gather_kernel(axis, x_ref, o_ref, own_sem, send_sems, recv_sems):
+    me, near, far = quad_peers(axis)
+    rows, width = x_ref.shape
+    part = rows // CHUNKS
+    meet([{axis: near}, {axis: far}])
+
+    def place(owner, at):
+        return o_ref.at[pl.ds(at * part, part), pl.ds(pl.multiple_of(owner * width, 128), width)]
+
+    def send(source, owner, at, slot, target):
+        copy = pltpu.make_async_remote_copy(
+            src_ref=source,
+            dst_ref=place(owner, at),
+            send_sem=send_sems.at[slot, at],
+            recv_sem=recv_sems.at[slot, at],
+            device_id={axis: target},
+            device_id_type=MESH_ID,
+        )
+        copy.start()
+        return copy
+
+    own = []
+    far_copies = []
+    for at in range(CHUNKS):
+        far_copies.append(send(x_ref.at[pl.ds(at * part, part)], me, at, 0, far))
+    for at in range(CHUNKS):
+        own.append(send(x_ref.at[pl.ds(at * part, part)], me, at, 1, near))
+    local = pltpu.make_async_copy(
+        x_ref, o_ref.at[:, pl.ds(pl.multiple_of(me * width, 128), width)], own_sem
+    )
+    local.start()
+    for at in range(CHUNKS):
+        far_copies[at].wait_recv()
+        own.append(send(place(far, at), far, at, 2, near))
+    for copy in far_copies:
+        copy.wait_send()
+    for copy in own:
+        copy.wait()
+    local.wait()
+
+
+def gather_columns(value, axis):
+    if lax.axis_size(axis) != 4:
+        return lax.all_gather(value, axis, axis=1, tiled=True)
+    rows, width = value.shape
+    return pl.pallas_call(
+        functools.partial(gather_kernel, axis),
+        out_shape=jax.ShapeDtypeStruct((rows, 4 * width), value.dtype),
+        in_specs=[VMEM_SPEC],
+        out_specs=VMEM_SPEC,
+        scratch_shapes=[
+            pltpu.SemaphoreType.DMA,
+            pltpu.SemaphoreType.DMA((3, CHUNKS)),
+            pltpu.SemaphoreType.DMA((3, CHUNKS)),
+        ],
+        compiler_params=pltpu.CompilerParams(
+            collective_id=2, has_side_effects=True, vmem_limit_bytes=16 << 20
+        ),
+        name="gather_columns",
+    )(value)
+
+
+def reduce_kernel(axis, n, quad, count, *refs):
+    refs = list(refs)
+    part_ref = refs.pop(0) if quad else None
+    grads = [refs.pop(0) for _ in range(count)]
+    up_ref = refs.pop(0) if quad else None
+    outs = [refs.pop(0) for _ in range(count)]
+    helds = [refs.pop(0) for _ in range(count)]
+    send_sems, recv_sems = refs.pop(0), refs.pop(0)
+    rank = lax.axis_index(axis)
+    peers = [lax.rem(rank + step, n) for step in range(1, n)]
+    targets = [{axis: peer} for peer in peers]
+    if quad:
+        near_buf, sum_buf, far_buf, quad_send, quad_recv = refs
+        me, near, far = quad_peers(quad)
+        targets = targets + [{quad: near}, {quad: far}]
+    meet(targets)
+    if quad:
+        rows = part_ref.shape[0]
+        width = part_ref.shape[1] // 4
+        part = rows // CHUNKS
+
+        def columns(owner):
+            return pl.ds(pl.multiple_of(owner * width, 128), width)
+
+        near_copies = [[], []]
+        for slot, owner in enumerate((lax.rem(near + 2, 4), near)):
+            for at in range(CHUNKS):
+                copy = pltpu.make_async_remote_copy(
+                    src_ref=part_ref.at[pl.ds(at * part, part), columns(owner)],
+                    dst_ref=near_buf.at[slot, pl.ds(at * part, part)],
+                    send_sem=quad_send.at[slot, at],
+                    recv_sem=quad_recv.at[slot, at],
+                    device_id={quad: near},
+                    device_id_type=MESH_ID,
+                )
+                copy.start()
+                near_copies[slot].append(copy)
+    grad_copies = []
+    for which in range(count):
+        block = outs[which].shape[0]
+        for step in range(1, n):
+            peer = peers[step - 1]
+            copy = pltpu.make_async_remote_copy(
+                src_ref=grads[which].at[pl.ds(pl.multiple_of(peer * block, 16), block)],
+                dst_ref=helds[which].at[step - 1],
+                send_sem=send_sems.at[which, step - 1],
+                recv_sem=recv_sems.at[which, step - 1],
+                device_id={axis: peer},
+                device_id_type=MESH_ID,
+            )
+            copy.start()
+            grad_copies.append(copy)
+    if quad:
+        stride = 64
+        far_copies = []
+        for at in range(CHUNKS):
+            near_copies[0][at].wait_recv()
+
+            @pl.loop(0, part // stride)
+            def _(line):
+                here = pl.ds(pl.multiple_of(at * part + line * stride, 16), stride)
+                sum_buf[here, :] = (
+                    part_ref[here, columns(far)].astype(jnp.float32)
+                    + near_buf[0, here, :].astype(jnp.float32)
+                ).astype(sum_buf.dtype)
+
+            copy = pltpu.make_async_remote_copy(
+                src_ref=sum_buf.at[pl.ds(at * part, part)],
+                dst_ref=far_buf.at[pl.ds(at * part, part)],
+                send_sem=quad_send.at[2, at],
+                recv_sem=quad_recv.at[2, at],
+                device_id={quad: far},
+                device_id_type=MESH_ID,
+            )
+            copy.start()
+            far_copies.append(copy)
+        for at in range(CHUNKS):
+            near_copies[1][at].wait_recv()
+            far_copies[at].wait_recv()
+
+            @pl.loop(0, part // stride)
+            def _(line):
+                here = pl.ds(pl.multiple_of(at * part + line * stride, 16), stride)
+                up_ref[here, :] = (
+                    part_ref[here, columns(me)].astype(jnp.float32)
+                    + near_buf[1, here, :].astype(jnp.float32)
+                    + far_buf[here, :].astype(jnp.float32)
+                )
+
+        for copy in near_copies[0] + near_copies[1] + far_copies:
+            copy.wait_send()
+    for copy in grad_copies:
+        copy.wait()
+    for which in range(count):
+        block = outs[which].shape[0]
+        stride = min(16, block)
+
+        @pl.loop(0, block // stride)
+        def _(line):
+            here = pl.ds(pl.multiple_of(line * stride, stride), stride)
+            mine = pl.ds(pl.multiple_of(rank * block + line * stride, stride), stride)
+            total = grads[which][mine, :].astype(jnp.float32)
+            for step in range(n - 1):
+                total = total + helds[which][step, here, :].astype(jnp.float32)
+            outs[which][here, :] = total
+
+
+def reduce_blocks(partial, grads, collective):
+    n = lax.axis_size("dp")
+    quad = "mp" if partial is not None else None
+    count = len(grads)
+    shapes = []
+    scratch = []
+    operands = []
+    if quad:
+        rows, width = partial.shape[0], partial.shape[1] // 4
+        operands.append(partial)
+        shapes.append(jax.ShapeDtypeStruct((rows, width), jnp.float32))
+    for grad in grads:
+        block = grad.shape[0] // n
+        operands.append(grad)
+        shapes.append(jax.ShapeDtypeStruct((block, grad.shape[1]), jnp.float32))
+        scratch.append(pltpu.VMEM((n - 1, block, grad.shape[1]), grad.dtype))
+    scratch += [pltpu.SemaphoreType.DMA((count, n - 1)), pltpu.SemaphoreType.DMA((count, n - 1))]
+    if quad:
+        scratch += [
+            pltpu.VMEM((2, rows, width), partial.dtype),
+            pltpu.VMEM((rows, width), partial.dtype),
+            pltpu.VMEM((rows, width), partial.dtype),
+            pltpu.SemaphoreType.DMA((3, CHUNKS)),
+            pltpu.SemaphoreType.DMA((3, CHUNKS)),
+        ]
+    return pl.pallas_call(
+        functools.partial(reduce_kernel, "dp", n, quad, count),
+        out_shape=shapes,
+        in_specs=[VMEM_SPEC] * len(operands),
+        out_specs=[VMEM_SPEC] * len(shapes),
+        scratch_shapes=scratch,
+        compiler_params=pltpu.CompilerParams(
+            collective_id=collective, has_side_effects=True, vmem_limit_bytes=32 << 20
+        ),
+        name="reduce_blocks",
+    )(*operands)
 
 
 def mish_act(values):
@@ -118,7 +348,7 @@
             whole_input = encoded
             summed = jnp.dot(whole_input, w_in, preferred_element_type=jnp.float32)
         else:
-            whole_input = lax.all_gather(current, "mp", axis=1, tiled=True)
+            whole_input = gather_columns(current, "mp")
             summed = jnp.dot(whole_input, w_mid[layer_at - 1], preferred_element_type=jnp.float32)
         full_inputs.append(whole_input)
         normed, inverse = column_stats(summed, batch_total)
@@ -126,14 +356,10 @@
         current = mish_act(shifted).astype(jnp.bfloat16)
         saved.append((normed, inverse, shifted))
     partial_out = jnp.dot(current, w_out, preferred_element_type=jnp.float32)
-    predicted = lax.psum(partial_out.astype(jnp.bfloat16), "mp").astype(jnp.float32)
+    predicted = exchange_sum(partial_out.astype(jnp.bfloat16), "mp", 1, "sum_output")
     residual_out = ((predicted - target) / math.sqrt(batch_total)).astype(jnp.bfloat16)
-    grad_out = lax.psum_scatter(
-        column_products(current, residual_out).astype(jnp.bfloat16),
-        "dp",
-        scatter_dimension=0,
-        tiled=True,
-    ).astype(jnp.float32)
+    waiting = [column_products(current, residual_out).astype(jnp.bfloat16)]
+    grad_out = None
     upstream = jnp.dot(residual_out, w_out.T, preferred_element_type=jnp.float32)
     grads_gain = []
     grads_bias = []
@@ -151,27 +377,21 @@
             * (slope_a - bias_sum / batch_total - normed * gain_sum / batch_total)
         ).astype(jnp.bfloat16)
         whole_input = full_inputs[layer_at]
-        if layer_at == 0:
-            grad_first = lax.psum_scatter(
-                column_products(whole_input, slope_z).astype(jnp.bfloat16),
-                "dp",
-                scatter_dimension=0,
-                tiled=True,
-            ).astype(jnp.float32)
+        waiting = [column_products(whole_input, slope_z).astype(jnp.bfloat16)] + waiting
+        partial_in = None
+        if layer_at > 0:
+            partial_in = jnp.dot(
+                slope_z, w_mid[layer_at - 1].T, preferred_element_type=jnp.float32
+            ).astype(jnp.bfloat16)
+        reduced = list(reduce_blocks(partial_in, waiting, 3 + layer_at))
+        if layer_at > 0:
+            upstream = reduced.pop(0)
+            grads_mid.append(reduced.pop(0))
         else:
-            grads_mid.append(
-                lax.psum_scatter(
-                    column_products(whole_input, slope_z).astype(jnp.bfloat16),
-                    "dp",
-                    scatter_dimension=0,
-                    tiled=True,
-                ).astype(jnp.float32)
-            )
-            weights = w_mid[layer_at - 1]
-            partial_in = jnp.dot(slope_z, weights.T, preferred_element_type=jnp.float32)
-            upstream = lax.psum_scatter(
-                partial_in.astype(jnp.bfloat16), "mp", scatter_dimension=1, tiled=True
-            ).astype(jnp.float32)
+            grad_first = reduced.pop(0)
+        if len(waiting) > 1:
+            grad_out = reduced.pop(0)
+        waiting = []
         grads_gain.append(gain_sum)
         grads_bias.append(bias_sum)
     grad_mid = jnp.stack(grads_mid[::-1])

time: 578 us -> 298 us (0.52)
  waiting for transfers between devices: 428 us -> 0 us
  Pallas kernels: 42.4 us -> 227 us
  matrix products: 46 us -> 26.6 us
  between operations: 14.2 us -> 1.14 us
  other arithmetic: 39.8 us -> 30.3 us
    reduce_scatter x6 -> x0, waiting for transfers between devices: 326 us -> none  [the longest x3 204 us: per_device(): lax.psum_scatter(column_products(whole_input, slope_z).astype(jnp.bfloat1...]
    pallas_call x6 -> x12, Pallas kernels: 42.4 us -> 227 us  [the longest x3 107 us: reduce_blocks(): pl.pallas_call(functools.partial(reduce_kernel, 'dp', n, quad, count), ou...]
    all_gather x2 -> x0, waiting for transfers between devices: 69.9 us -> none  [per_device(): whole_input = lax.all_gather(current, 'mp', axis=1, tiled=True)]
    psum x1 -> x0, waiting for transfers between devices: 31.6 us -> none  [per_device(): lax.psum(partial_out.astype(jnp.bfloat16), 'mp').astype(jnp.float32)]
    dot_general x4, matrix products: 17.7 us -> 8.84 us  [column_products(): return jnp.dot(left_rows.T, right_rows, preferred_element_type=jnp.float32)]
  transfers between devices with their start and end apart: 9 -> 0, of which waited for: 9 -> 0; matrix products, arithmetic and copies ran while one was open for 5% -> 0% of each run, Pallas kernels for 1% -> 0%
where the time goes in v2:
time: 298 us; the launch traced here: 293 us
  Pallas kernels  227 us (76%)
  other arithmetic  30.3 us (10%)
  matrix products  26.6 us (9%)
  local copies, waits for them, and re-layouts  7.27 us (2%)
    pallas_call x3, Pallas kernels, reduce_blocks(): pl.pallas_call(functools.partial(reduce_kernel, 'dp', n, quad, count), ou...  107 us
    pallas_call x7, Pallas kernels, exchange_sum(): pl.pallas_call(functools.partial(exchange_kernel, axis, n), out_shape=jax...  67.4 us
    pallas_call x2, Pallas kernels, gather_columns(): pl.pallas_call(functools.partial(gather_kernel, axis), out_shape=jax.Shap...  52.5 us
    dot_general x4, matrix products, column_products(): return jnp.dot(left_rows.T, right_rows, preferred_element_type=jnp.float32)  8.84 us
    reduce_sum x2, other arithmetic, per_device(): jnp.sum(slope_a, axis=0)  7.32 us
    convert_element_type x3, other arithmetic, per_device(): current = mish_act(shifted).astype(jnp.bfloat16)  6.25 us
    dot_general x2, matrix products, per_device(): jnp.dot(whole_input, w_mid[layer_at - 1], preferred_element_type=jnp.floa...  6.01 us

profile of v2, /device:TPU:0, one launch (start us, length us, event | category | flops | bytes accessed | tf_op | source)
XLA Modules:
  0.0 292.6 jit_solution(2443026684435050338)
XLA Ops:
  0.6 0.0 copy-start
  0.6 0.8 convert_element_type.69
  1.4 0.7 convert_element_type.71
  2.1 0.7 convert_element_type.70
  2.8 0.8 fusion.42
  3.6 0.8 fusion.41
  4.4 0.8 convert_divide_fusion
  5.2 2.0 copy.20
  7.1 5.4 %add_convert_fusion = bf16[1024,1024]{1,0:T(8,128)(2,1)S(1)} fusion(f32[1024]{0:T(1024)S(1)} %get-tuple-element.15, f32[1024]{0:T(1024)S(1)} %convert_element_type.71, f32[1024]{0:T(1024)S(1)} %get-tuple-element.14, f32[1024]{0:T(1024)S(1)} %convert_element_type.70, s32[1024]{0:T(1024)} %param.13, s32[1024]{0:T(1024)} %param.14, ...), kind=kLoop, calls=%fused_computation.5 | loop fusion | flops 28311552 | bytes 2138112 | tf_op jit(solution)/shard_map/convert_element_type | solution.py:30
  12.5 0.0 copy-done
  12.5 0.0 copy-start.10
  12.5 1.3 fusion.40
  13.8 0.1 copy-done.10
  14.0 8.6 %sum_pair.6 = f32[8,128]{1,0:T(8,128)S(1)} custom-call(f32[8,128]{1,0:T(8,128)S(1)} %reshape.242.x_ref), custom_call_target="tpu_custom_call" | custom-call | tf_op jit(solution)/shard_map/sum_pair/pallas_call | solution.py:67
  22.5 1.5 fusion.10.x_ref
  24.1 0.0 copy-done.7
  24.1 0.0 copy-start.14
  24.1 26.7 %gather_columns.2 = bf16[1024,2048]{1,0:T(8,128)(2,1)S(1)} custom-call(bf16[1024,512]{1,0:T(8,128)(2,1)S(1)} %fusion.10.x_ref), custom_call_target="tpu_custom_call" | custom-call | tf_op jit(solution)/shard_map/gather_columns/pallas_call | solution.py:154
  50.8 0.0 copy-done.14
  50.9 2.3 fusion.39
  53.3 6.7 %sum_pair.7 = f32[8,128]{1,0:T(8,128)S(1)} custom-call(f32[8,128]{1,0:T(8,128)S(1)} %reshape.243.x_ref), custom_call_target="tpu_custom_call" | custom-call | tf_op jit(solution)/shard_map/sum_pair/pallas_call | solution.py:67
  60.0 1.5 fusion.12.x_ref
  61.5 0.0 copy-start.15
  61.5 25.8 %gather_columns.3 = bf16[1024,2048]{1,0:T(8,128)(2,1)S(1)} custom-call(bf16[1024,512]{1,0:T(8,128)(2,1)S(1)} %fusion.12.x_ref), custom_call_target="tpu_custom_call" | custom-call | tf_op jit(solution)/shard_map/gather_columns/pallas_call | solution.py:154
  87.4 0.0 copy-start.13
  87.4 3.7 %fusion.38 = (f32[512]{0:T(512)S(1)}, f32[512]{0:T(512)S(1)}, f32[1024,512]{1,0:T(8,128)}) fusion(bf16[1024,2048]{1,0:T(8,128)(2,1)S(1)} %gather_columns.3, bf16[2,2048,512]{2,1,0:T(8,128)(2,1)S(1)} %copy-done.15), kind=kOutput, calls=%fused_computation.106 | convolution fusion | flops 2149055488 | bytes 8392704 | tf_op jit(solution)/shard_map/dot_general | solution.py:352
  91.1 6.6 %sum_pair.8 = f32[8,128]{1,0:T(8,128)S(1)} custom-call(f32[8,128]{1,0:T(8,128)S(1)} %reshape.244.x_ref), custom_call_target="tpu_custom_call" | custom-call | tf_op jit(solution)/shard_map/sum_pair/pallas_call | solution.py:67
  97.8 0.0 copy-start.11
  97.8 3.2 %fusion.14 = bf16[1024,512]{1,0:T(8,128)(2,1)S(1)} fusion(f32[1024,512]{1,0:T(8,128)} %get-tuple-element.66, f32[512]{0:T(512)S(1)} %bitcast.119, f32[512]{0:T(512)S(1)} %fusion.26, f32[512]{0:T(512)S(1)} %get-tuple-element.61, f32[512]{0:T(512)S(1)} %bitcast.117), kind=kLoop, calls=%fused_computation.33 | loop fusion | flops 6291456 | bytes 3153920 | tf_op jit(solution)/shard_map/convert_element_type | solution.py:356
  101.0 0.0 copy-done.12
  101.0 0.4 convolution_convert_fusion.5
  101.4 0.2 copy.19.x_ref
  101.6 13.5 %sum_output.1 = f32[1024,64]{1,0:T(8,128)S(1)} custom-call(bf16[1024,64]{1,0:T(8,128)(2,1)S(1)} %copy.19.x_ref), custom_call_target="tpu_custom_call" | custom-call | tf_op jit(solution)/shard_map/sum_output/pallas_call | solution.py:67
  115.1 0.0 copy-done.11
  115.1 0.1 multiply_convert_fusion.4
  115.2 0.3 convolution_convert_fusion.6
  115.5 0.1 copy.21.refs_2_
  115.7 5.3 %fusion.37 = (f32[512]{0:T(512)S(1)}, f32[512]{0:T(512)S(1)}, f32[1024,512]{1,0:T(8,128)}) fusion(f32[512]{0:T(512)S(1)} %fusion.26, f32[1024,512]{1,0:T(8,128)} %get-tuple-element.66, f32[512]{0:T(512)S(1)} %get-tuple-element.61, f32[512]{0:T(512)S(1)} %bitcast.120, f32[512]{0:T(512)S(1)} %bitcast.118, bf16[1024,64]{1,0:T(8,128)(2,1)S(1)} %multiply_convert_fusion.4, ...), kind=kOutput, calls=%fused_computation.105 | convolution fusion | flops 78642176 | bytes 4403200 | tf_op jit(solution)/shard_map/dot_general | solution.py:363
  121.0 6.9 %sum_pair.9 = f32[8,128]{1,0:T(8,128)S(1)} custom-call(f32[8,128]{1,0:T(8,128)S(1)} %reshape.245.x_ref), custom_call_target="tpu_custom_call" | custom-call | tf_op jit(solution)/shard_map/sum_pair/pallas_call | solution.py:67
  127.9 3.0 %multiply_convert_fusion.2 = bf16[1024,512]{1,0:T(8,128)(2,1)S(1)} fusion(f32[1024,512]{1,0:T(8,128)} %get-tuple-element.67, f32[1024,512]{1,0:T(8,128)} %get-tuple-element.66, f32[512]{0:T(512)S(1)} %get-tuple-element.54, f32[512]{0:T(512)S(1)} %get-tuple-element.53, f32[512]{0:T(512)S(1)} %fusion.26, f32[512]{0:T(512)S(1)} %get-tuple-element.61, ...), kind=kLoop, calls=%fused_computation.29 | loop fusion | flops 4194304 | bytes 5253120 | tf_op jit(solution)/shard_map/convert_element_type | solution.py:378
  130.9 0.5 copy-done.4
  131.4 2.4 convolution_convert_fusion.3.refs_1_
  133.8 2.4 convolution_convert_fusion.1.refs_0_
  136.2 53.4 %reduce_blocks.3 = (f32[1024,512]{1,0:T(8,128)S(1)}, f32[256,512]{1,0:T(8,128)S(1)}, f32[64,64]{1,0:T(8,128)S(1)}) custom-call(bf16[1024,2048]{1,0:T(8,128)(2,1)S(1)} %convolution_convert_fusion.1.refs_0_, bf16[2048,512]{1,0:T(8,128)(2,1)S(1)} %convolution_convert_fusion.3.refs_1_, bf16[512,64]{1,0:T(8,128)(2,1)S(1)} %copy.21.refs_2_), custom_call_target="tpu_custom_call" | custom-call | tf_op jit(solution)/shard_map/reduce_blocks/pallas_call | solution.py:303
  189.7 3.6 %fusion.36 = (f32[512]{0:T(512)S(1)}, f32[512]{0:T(512)S(1)}, f32[1024,512]{1,0:T(8,128)}) fusion(f32[512]{0:T(512)S(1)} %fusion.28, f32[1024,512]{1,0:T(8,128)S(1)} %copy-done.6, f32[512]{0:T(512)S(1)} %get-tuple-element.59, f32[1024,512]{1,0:T(8,128)S(1)} %get-tuple-element.16, f32[512]{0:T(512)S(1)} %bitcast.114, f32[512]{0:T(512)S(1)} %bitcast.112), kind=kLoop, calls=%fused_computation.104 | loop fusion | flops 11533312 | bytes 6303744 | tf_op jit(solution)/shard_map/reduce_sum | solution.py:372
  193.3 6.5 %sum_pair.10 = f32[8,128]{1,0:T(8,128)S(1)} custom-call(f32[8,128]{1,0:T(8,128)S(1)} %reshape.246.x_ref), custom_call_target="tpu_custom_call" | custom-call | tf_op jit(solution)/shard_map/sum_pair/pallas_call | solution.py:67
  199.9 0.0 copy-start.2
  199.9 3.0 %multiply_convert_fusion.1 = bf16[1024,512]{1,0:T(8,128)(2,1)S(1)} fusion(f32[1024,512]{1,0:T(8,128)} %get-tuple-element.34, f32[1024,512]{1,0:T(8,128)} %copy-done.5, f32[512]{0:T(512)S(1)} %get-tuple-element.50, f32[512]{0:T(512)S(1)} %get-tuple-element.49, f32[512]{0:T(512)S(1)} %fusion.28, f32[512]{0:T(512)S(1)} %get-tuple-element.59, f32[512]{0:T(512)S(1)} %bitcast.115), kind=kLoop, calls=%fused_computation.24 | loop fusion | flops 4194304 | bytes 5253120 | tf_op jit(solution)/shard_map/convert_element_type | solution.py:378
  202.9 0.5 copy-done.2
  203.3 2.4 convolution_convert_fusion.2.refs_1_
  205.8 2.4 convolution_convert_fusion.refs_0_
  208.2 36.1 %reduce_blocks.4 = (f32[1024,512]{1,0:T(8,128)S(1)}, f32[256,512]{1,0:T(8,128)S(1)}) custom-call(bf16[1024,2048]{1,0:T(8,128)(2,1)S(1)} %convolution_convert_fusion.refs_0_, bf16[2048,512]{1,0:T(8,128)(2,1)S(1)} %convolution_convert_fusion.2.refs_1_), custom_call_target="tpu_custom_call" | custom-call | tf_op jit(solution)/shard_map/reduce_blocks/pallas_call | solution.py:303
  244.3 0.0 copy-start.8
  244.3 1.0 pad_maximum_fusion
  245.3 0.9 copy-done.8
  246.2 3.7 %fusion.35 = (f32[512]{0:T(512)S(1)}, f32[512]{0:T(512)S(1)}, f32[1024,512]{1,0:T(8,128)}) fusion(f32[512]{0:T(512)S(1)} %fusion.30, f32[1024,512]{1,0:T(8,128)S(1)} %copy-done.8, f32[512]{0:T(512)S(1)} %get-tuple-element.57, f32[1024,512]{1,0:T(8,128)S(1)} %get-tuple-element.17, f32[512]{0:T(512)S(1)} %bitcast.110, f32[512]{0:T(512)S(1)} %bitcast.108), kind=kLoop, calls=%fused_computation.103 | loop fusion | flops 11533312 | bytes 6303744 | tf_op jit(solution)/shard_map/reduce_sum | solution.py:372
  249.9 18.7 %sum_pair.11 = f32[8,128]{1,0:T(8,128)S(1)} custom-call(f32[8,128]{1,0:T(8,128)S(1)} %reshape.247.x_ref), custom_call_target="tpu_custom_call" | custom-call | tf_op jit(solution)/shard_map/sum_pair/pallas_call | solution.py:67
  268.6 0.0 copy-done.9
  268.6 3.6 %convolution_convert_fusion.4.refs_0_ = bf16[1024,512]{1,0:T(8,128)(2,1)S(1)} fusion(bf16[1024,1024]{1,0:T(8,128)(2,1)} %copy-done.10, f32[1024,512]{1,0:T(8,128)} %get-tuple-element.33, f32[1024,512]{1,0:T(8,128)S(1)} %copy-done.9, f32[512]{0:T(512)S(1)} %get-tuple-element.46, f32[512]{0:T(512)S(1)} %get-tuple-element.45, f32[512]{0:T(512)S(1)} %fusion.30, ...), kind=kOutput, calls=%fused_computation.50 | convolution fusion | flops 1078460416 | bytes 7350272 | tf_op jit(solution)/shard_map/dot_general | solution.py:335
  272.3 17.8 %reduce_blocks.5 = f32[128,512]{1,0:T(8,128)S(1)} custom-call(bf16[1024,512]{1,0:T(8,128)(2,1)S(1)} %convolution_convert_fusion.4.refs_0_), custom_call_target="tpu_custom_call" | custom-call | tf_op jit(solution)/shard_map/reduce_blocks/pallas_call | solution.py:303
  290.1 0.6 pad_maximum_fusion.2
  290.7 0.6 pad_maximum_fusion.1
  291.3 0.7 copy.24
  292.0 0.6 copy.25
  (40 shorter events, 0.2 us)
Async XLA Ops:
  0.6 11.9 %copy-start = (bf16[1024,512]{1,0:T(8,128)(2,1)S(1)}, bf16[1024,512]{1,0:T(8,128)(2,1)}, u32[]{:S(2)}) copy-start(bf16[1024,512]{1,0:T(8,128)(2,1)} %param.16) | copy-start | bytes 3145732
  12.5 1.4 copy-start.10
  13.9 10.2 %copy-start.7 = (f32[1024,512]{1,0:T(8,128)}, f32[1024,512]{1,0:T(8,128)S(1)}, u32[]{:S(2)}) copy-start(f32[1024,512]{1,0:T(8,128)S(1)} %get-tuple-element.64) | copy-start | bytes 6291460
  24.1 26.7 %copy-start.14 = (bf16[2,2048,512]{2,1,0:T(8,128)(2,1)S(1)}, bf16[2,2048,512]{2,1,0:T(8,128)(2,1)}, u32[]{:S(2)}) copy-start(bf16[2,2048,512]{2,1,0:T(8,128)(2,1)} %param.17) | copy-start | bytes 12582916
  50.9 2.4 copy-start.1
  53.2 34.2 %copy-start.5 = (f32[1024,512]{1,0:T(8,128)}, f32[1024,512]{1,0:T(8,128)S(1)}, u32[]{:S(2)}) copy-start(f32[1024,512]{1,0:T(8,128)S(1)} %get-tuple-element.65) | copy-start | bytes 6291460
  61.5 25.9 %copy-start.15 = (bf16[2,2048,512]{2,1,0:T(8,128)(2,1)S(1)}, bf16[2,2048,512]{2,1,0:T(8,128)(2,1)}, u32[]{:S(2)}) copy-start(bf16[2,2048,512]{2,1,0:T(8,128)(2,1)} %param.17) | copy-start | bytes 12582916
  87.4 3.7 %copy-start.3 = (bf16[1024,2048]{1,0:T(8,128)(2,1)}, bf16[1024,2048]{1,0:T(8,128)(2,1)S(1)}, u32[]{:S(2)}) copy-start(bf16[1024,2048]{1,0:T(8,128)(2,1)S(1)} %gather_columns.3) | copy-start | bytes 12582916
  87.4 10.4 %copy-start.13 = (f32[3,512]{1,0:T(4,128)S(1)}, f32[3,512]{1,0:T(4,128)}, u32[]{:S(2)}) copy-start(f32[3,512]{1,0:T(4,128)} %param.19) | copy-start | bytes 18436
  91.1 9.9 %copy-start.12 = (bf16[512,64]{0,1:T(8,128)(2,1)S(1)}, bf16[512,64]{0,1:T(8,128)(2,1)}, u32[]{:S(2)}) copy-start(bf16[512,64]{0,1:T(8,128)(2,1)} %param.18) | copy-start | bytes 196612
  97.8 17.3 %copy-start.11 = (f32[1024,64]{1,0:T(8,128)S(1)}, f32[1024,64]{1,0:T(8,128)}, u32[]{:S(2)}) copy-start(f32[1024,64]{1,0:T(8,128)} %copy.20) | copy-start | bytes 786436
  127.9 3.5 %copy-start.4 = (bf16[1024,2048]{1,0:T(8,128)(2,1)S(1)}, bf16[1024,2048]{1,0:T(8,128)(2,1)}, u32[]{:S(2)}) copy-start(bf16[1024,2048]{1,0:T(8,128)(2,1)} %copy-done.3) | copy-start | bytes 12582916
  131.4 2.5 copy-start.16
  136.2 53.4 %copy-start.6 = (f32[1024,512]{1,0:T(8,128)S(1)}, f32[1024,512]{1,0:T(8,128)}, u32[]{:S(2)}) copy-start(f32[1024,512]{1,0:T(8,128)} %copy-done.5) | copy-start | bytes 6291460
  199.9 3.5 %copy-start.2 = (bf16[1024,2048]{1,0:T(8,128)(2,1)S(1)}, bf16[1024,2048]{1,0:T(8,128)(2,1)}, u32[]{:S(2)}) copy-start(bf16[1024,2048]{1,0:T(8,128)(2,1)} %copy-done.1) | copy-start | bytes 12582916
  203.3 2.5 copy-start.17
  244.3 2.0 copy-start.8
  246.2 22.4 %copy-start.9 = (f32[1024,512]{1,0:T(8,128)S(1)}, f32[1024,512]{1,0:T(8,128)}, u32[]{:S(2)}) copy-start(f32[1024,512]{1,0:T(8,128)} %copy-done.7) | copy-start | bytes 6291460

commit v3 on v2

--- a/solution.py
+++ b/solution.py
@@ -175,10 +175,15 @@
     up_ref = refs.pop(0) if quad else None
     outs = [refs.pop(0) for _ in range(count)]
     helds = [refs.pop(0) for _ in range(count)]
+    pairs = [refs.pop(0) for _ in range(count)]
+    sums = [refs.pop(0) for _ in range(count)]
     send_sems, recv_sems = refs.pop(0), refs.pop(0)
     rank = lax.axis_index(axis)
-    peers = [lax.rem(rank + step, n) for step in range(1, n)]
-    targets = [{axis: peer} for peer in peers]
+    half = n // 2
+    beside = rank + 1 - 2 * lax.rem(rank, 2)
+    turn = beside - rank
+    peers = [lax.rem(rank + 2 * step, n) for step in range(1, half)]
+    targets = [{axis: beside}] + [{axis: peer} for peer in peers]
     if quad:
         near_buf, sum_buf, far_buf, quad_send, quad_recv = refs
         me, near, far = quad_peers(quad)
@@ -205,21 +210,23 @@
                 )
                 copy.start()
                 near_copies[slot].append(copy)
-    grad_copies = []
+    pair_copies = []
     for which in range(count):
         block = outs[which].shape[0]
-        for step in range(1, n):
-            peer = peers[step - 1]
+        copies = []
+        for slot in [*range(1, half), 0]:
+            owner = lax.rem(rank + 2 * slot, n) + turn
             copy = pltpu.make_async_remote_copy(
-                src_ref=grads[which].at[pl.ds(pl.multiple_of(peer * block, 16), block)],
-                dst_ref=helds[which].at[step - 1],
-                send_sem=send_sems.at[which, step - 1],
-                recv_sem=recv_sems.at[which, step - 1],
-                device_id={axis: peer},
+                src_ref=grads[which].at[pl.ds(pl.multiple_of(owner * block, 16), block)],
+                dst_ref=pairs[which].at[slot],
+                send_sem=send_sems.at[which, 0, slot],
+                recv_sem=recv_sems.at[which, 0, slot],
+                device_id={axis: beside},
                 device_id_type=MESH_ID,
             )
             copy.start()
-            grad_copies.append(copy)
+            copies.append(copy)
+        pair_copies.append(copies)
     if quad:
         stride = 64
         far_copies = []
@@ -244,6 +251,35 @@
             )
             copy.start()
             far_copies.append(copy)
+
+    grad_copies = []
+    for which in range(count):
+        block = outs[which].shape[0]
+        stride = min(16, block)
+        for step in range(1, half):
+            pair_copies[which][step - 1].wait_recv()
+            peer = peers[step - 1]
+
+            @pl.loop(0, block // stride)
+            def _(line):
+                here = pl.ds(pl.multiple_of(line * stride, stride), stride)
+                theirs = pl.ds(pl.multiple_of(peer * block + line * stride, stride), stride)
+                sums[which][step - 1, here, :] = (
+                    grads[which][theirs, :].astype(jnp.float32)
+                    + pairs[which][step, here, :].astype(jnp.float32)
+                ).astype(sums[which].dtype)
+
+            copy = pltpu.make_async_remote_copy(
+                src_ref=sums[which].at[step - 1],
+                dst_ref=helds[which].at[step - 1],
+                send_sem=send_sems.at[which, 1, step - 1],
+                recv_sem=recv_sems.at[which, 1, step - 1],
+                device_id={axis: peer},
+                device_id_type=MESH_ID,
+            )
+            copy.start()
+            grad_copies.append(copy)
+    if quad:
         for at in range(CHUNKS):
             near_copies[1][at].wait_recv()
             far_copies[at].wait_recv()
@@ -259,6 +295,10 @@
 
         for copy in near_copies[0] + near_copies[1] + far_copies:
             copy.wait_send()
+    for which in range(count):
+        pair_copies[which][half - 1].wait_recv()
+        for copy in pair_copies[which]:
+            copy.wait_send()
     for copy in grad_copies:
         copy.wait()
     for which in range(count):
@@ -270,7 +310,8 @@
             here = pl.ds(pl.multiple_of(line * stride, stride), stride)
             mine = pl.ds(pl.multiple_of(rank * block + line * stride, stride), stride)
             total = grads[which][mine, :].astype(jnp.float32)
-            for step in range(n - 1):
+            total = total + pairs[which][0, here, :].astype(jnp.float32)
+            for step in range(half - 1):
                 total = total + helds[which][step, here, :].astype(jnp.float32)
             outs[which][here, :] = total
 
@@ -290,8 +331,11 @@
         block = grad.shape[0] // n
         operands.append(grad)
         shapes.append(jax.ShapeDtypeStruct((block, grad.shape[1]), jnp.float32))
-        scratch.append(pltpu.VMEM((n - 1, block, grad.shape[1]), grad.dtype))
-    scratch += [pltpu.SemaphoreType.DMA((count, n - 1)), pltpu.SemaphoreType.DMA((count, n - 1))]
+    half = n // 2
+    for slots in (half - 1, half, half - 1):
+        for grad in grads:
+            scratch.append(pltpu.VMEM((slots, grad.shape[0] // n, grad.shape[1]), grad.dtype))
+    scratch += [pltpu.SemaphoreType.DMA((count, 2, half))] * 2
     if quad:
         scratch += [
             pltpu.VMEM((2, rows, width), partial.dtype),
@@ -313,13 +357,27 @@
     )(*operands)
 
 
+def mish_parts(values):
+    small = jnp.exp(-jnp.abs(values))
+    upper = values >= 0.0
+    top = jnp.where(upper, 1.0 + 2.0 * small, small * (small + 2.0))
+    rest = jnp.where(upper, 2.0 * small * small, 2.0)
+    return small, upper, top, rest
+
+
 def mish_act(values):
-    return values * jnp.tanh(jax.nn.softplus(values))
+    _, _, top, rest = mish_parts(values)
+    return values * (top / (top + rest))
 
 
 def mish_slope(values):
-    tangent = jnp.tanh(jax.nn.softplus(values))
-    return tangent + values * (1.0 - tangent * tangent) * jax.nn.sigmoid(values)
+    small, upper, top, rest = mish_parts(values)
+    whole = top + rest
+    inverse = 1.0 / (whole * (1.0 + small))
+    each = inverse * (1.0 + small)
+    tangent = top * each
+    logistic = jnp.where(upper, 1.0, small) * (inverse * whole)
+    return tangent + values * (rest * each) * (1.0 + tangent) * logistic
 
 
 def column_stats(summed, batch_total):
@@ -355,8 +413,8 @@
         shifted = bn_gain[layer_at] * normed + bn_bias[layer_at]
         current = mish_act(shifted).astype(jnp.bfloat16)
         saved.append((normed, inverse, shifted))
-    partial_out = jnp.dot(current, w_out, preferred_element_type=jnp.float32)
-    predicted = exchange_sum(partial_out.astype(jnp.bfloat16), "mp", 1, "sum_output")
+    partial_out = jnp.dot(current, w_out, preferred_element_type=jnp.float32).T
+    predicted = exchange_sum(partial_out.astype(jnp.bfloat16), "mp", 1, "sum_output").T
     residual_out = ((predicted - target) / math.sqrt(batch_total)).astype(jnp.bfloat16)
     waiting = [column_products(current, residual_out).astype(jnp.bfloat16)]
     grad_out = None

time: 298 us -> 251 us (0.84); the launches traced: 293 us -> 250 us
  Pallas kernels: 227 us -> 188 us
    pallas_call x3, Pallas kernels: 107 us -> 84.1 us  [reduce_blocks(): pl.pallas_call(functools.partial(reduce_kernel, 'dp', n, quad, count), ou...]
    pallas_call x7, Pallas kernels: 67.4 us -> 51.7 us  [exchange_sum(): pl.pallas_call(functools.partial(exchange_kernel, axis, n), out_shape=jax...]
where the time goes in v3:
time: 251 us; the launch traced here: 250 us
  Pallas kernels  188 us (75%)
  other arithmetic  29.2 us (12%)
  matrix products  26.4 us (11%)
  local copies, waits for them, and re-layouts  5.15 us (2%)
    pallas_call x3, Pallas kernels, reduce_blocks(): pl.pallas_call(functools.partial(reduce_kernel, 'dp', n, quad, count), ou...  84.1 us
    pallas_call x2, Pallas kernels, gather_columns(): pl.pallas_call(functools.partial(gather_kernel, axis), out_shape=jax.Shap...  52.5 us
    pallas_call x7, Pallas kernels, exchange_sum(): pl.pallas_call(functools.partial(exchange_kernel, axis, n), out_shape=jax...  51.7 us
    dot_general x4, matrix products, column_products(): return jnp.dot(left_rows.T, right_rows, preferred_element_type=jnp.float32)  8.81 us
    reduce_sum x2, other arithmetic, per_device(): jnp.sum(slope_a, axis=0)  6.85 us
    dot_general x2, matrix products, per_device(): jnp.dot(whole_input, w_mid[layer_at - 1], preferred_element_type=jnp.floa...  6.03 us
    convert_element_type x2, other arithmetic, per_device(): slope_z = (bn_gain[layer_at] * inverse * (slope_a - bias_sum / batch_tota...  5.93 us
    convert_element_type x3, other arithmetic, per_device(): current = mish_act(shifted).astype(jnp.bfloat16)  5.63 us

profile of v3, /device:TPU:0, one launch (start us, length us, event | category | flops | bytes accessed | tf_op | source)
XLA Modules:
  0.0 250.2 jit_solution(5903229332478729988)
XLA Ops:
  0.6 0.0 copy-start
  0.6 0.8 convert_element_type.71
  1.4 0.7 convert_element_type.73
  2.1 0.7 convert_element_type.72
  2.8 0.8 fusion.48
  3.6 0.8 fusion.47
  4.4 0.8 convert_divide_fusion
  5.2 5.4 %add_convert_fusion = bf16[1024,1024]{1,0:T(8,128)(2,1)S(1)} fusion(f32[1024]{0:T(1024)S(1)} %get-tuple-element.15, f32[1024]{0:T(1024)S(1)} %convert_element_type.73, f32[1024]{0:T(1024)S(1)} %get-tuple-element.14, f32[1024]{0:T(1024)S(1)} %convert_element_type.72, s32[1024]{0:T(1024)} %param.13, s32[1024]{0:T(1024)} %param.14, ...), kind=kLoop, calls=%fused_computation.2 | loop fusion | flops 28311552 | bytes 2138112 | tf_op jit(solution)/shard_map/convert_element_type | solution.py:30
  10.6 0.0 copy-done
  10.6 0.0 copy-start.10
  10.6 1.3 fusion.46
  11.9 0.1 copy-done.10
  12.0 8.6 %sum_pair.6 = f32[8,128]{1,0:T(8,128)S(1)} custom-call(f32[8,128]{1,0:T(8,128)S(1)} %reshape.242.x_ref), custom_call_target="tpu_custom_call" | custom-call | tf_op jit(solution)/shard_map/sum_pair/pallas_call | solution.py:67
  20.6 1.3 fusion.17.x_ref
  21.9 0.0 copy-done.7
  21.9 0.0 copy-start.14
  22.0 26.7 %gather_columns.2 = bf16[1024,2048]{1,0:T(8,128)(2,1)S(1)} custom-call(bf16[1024,512]{1,0:T(8,128)(2,1)S(1)} %fusion.17.x_ref), custom_call_target="tpu_custom_call" | custom-call | tf_op jit(solution)/shard_map/gather_columns/pallas_call | solution.py:154
  48.7 0.0 copy-done.14
  48.7 0.0 copy-start.1
  48.7 2.3 fusion.45
  51.1 0.0 copy-done.1
  51.1 6.7 %sum_pair.7 = f32[8,128]{1,0:T(8,128)S(1)} custom-call(f32[8,128]{1,0:T(8,128)S(1)} %reshape.243.x_ref), custom_call_target="tpu_custom_call" | custom-call | tf_op jit(solution)/shard_map/sum_pair/pallas_call | solution.py:67
  57.9 1.3 fusion.16.x_ref
  59.2 0.0 copy-start.15
  59.2 25.8 %gather_columns.3 = bf16[1024,2048]{1,0:T(8,128)(2,1)S(1)} custom-call(bf16[1024,512]{1,0:T(8,128)(2,1)S(1)} %fusion.16.x_ref), custom_call_target="tpu_custom_call" | custom-call | tf_op jit(solution)/shard_map/gather_columns/pallas_call | solution.py:154
  85.0 0.0 copy-done.5
  85.0 0.0 copy-done.15
  85.0 0.0 copy-start.3
  85.1 0.0 copy-start.13
  85.1 3.7 %fusion.44 = (f32[512]{0:T(512)S(1)}, f32[512]{0:T(512)S(1)}, f32[1024,512]{1,0:T(8,128)}) fusion(bf16[1024,2048]{1,0:T(8,128)(2,1)S(1)} %gather_columns.3, bf16[2,2048,512]{2,1,0:T(8,128)(2,1)S(1)} %copy-done.15), kind=kOutput, calls=%fused_computation.121 | convolution fusion | flops 2149055488 | bytes 8392704 | tf_op jit(solution)/shard_map/dot_general | solution.py:410
  88.8 6.6 %sum_pair.8 = f32[8,128]{1,0:T(8,128)S(1)} custom-call(f32[8,128]{1,0:T(8,128)S(1)} %reshape.244.x_ref), custom_call_target="tpu_custom_call" | custom-call | tf_op jit(solution)/shard_map/sum_pair/pallas_call | solution.py:67
  95.4 0.0 copy-done.13
  95.4 0.0 copy-start.11
  95.5 3.0 %fusion.15 = bf16[1024,512]{1,0:T(8,128)(2,1)S(1)} fusion(f32[1024,512]{1,0:T(8,128)} %get-tuple-element.66, f32[512]{0:T(512)S(1)} %bitcast.127, f32[512]{0:T(512)S(1)} %fusion.32, f32[512]{0:T(512)S(1)} %get-tuple-element.61, f32[512]{0:T(512)S(1)} %bitcast.125), kind=kLoop, calls=%fused_computation.55 | loop fusion | flops 9437184 | bytes 3153920 | tf_op jit(solution)/shard_map/convert_element_type | solution.py:414
  98.4 0.0 copy-done.12
  98.4 0.4 fusion.22.x_ref
  98.9 7.8 %sum_output.1 = f32[64,1024]{1,0:T(8,128)S(1)} custom-call(bf16[64,1024]{1,0:T(8,128)(2,1)S(1)} %fusion.22.x_ref), custom_call_target="tpu_custom_call" | custom-call | tf_op jit(solution)/shard_map/sum_output/pallas_call | solution.py:67
  106.7 0.3 convolution_convert_fusion.6
  107.1 0.1 copy.17.refs_2_
  107.2 5.1 %fusion.43 = (f32[512]{0:T(512)S(1)}, f32[512]{0:T(512)S(1)}, f32[1024,512]{1,0:T(8,128)}) fusion(f32[512]{0:T(512)S(1)} %fusion.32, f32[1024,512]{1,0:T(8,128)} %get-tuple-element.66, f32[512]{0:T(512)S(1)} %get-tuple-element.61, f32[512]{0:T(512)S(1)} %bitcast.128, f32[512]{0:T(512)S(1)} %bitcast.126, bf16[1024,64]{0,1:T(8,128)(2,1)S(1)} %fusion.30, ...), kind=kOutput, calls=%fused_computation.120 | convolution fusion | flops 84409344 | bytes 4403200 | tf_op jit(solution)/shard_map/dot_general | solution.py:421
  112.3 6.9 %sum_pair.9 = f32[8,128]{1,0:T(8,128)S(1)} custom-call(f32[8,128]{1,0:T(8,128)S(1)} %reshape.245.x_ref), custom_call_target="tpu_custom_call" | custom-call | tf_op jit(solution)/shard_map/sum_pair/pallas_call | solution.py:67
  119.2 0.0 copy-start.4
  119.2 3.0 %multiply_convert_fusion.2 = bf16[1024,512]{1,0:T(8,128)(2,1)S(1)} fusion(f32[1024,512]{1,0:T(8,128)} %get-tuple-element.67, f32[1024,512]{1,0:T(8,128)} %get-tuple-element.66, f32[512]{0:T(512)S(1)} %get-tuple-element.54, f32[512]{0:T(512)S(1)} %get-tuple-element.53, f32[512]{0:T(512)S(1)} %fusion.32, f32[512]{0:T(512)S(1)} %get-tuple-element.61, ...), kind=kLoop, calls=%fused_computation.38 | loop fusion | flops 4194304 | bytes 5253120 | tf_op jit(solution)/shard_map/convert_element_type | solution.py:436
  122.2 0.5 copy-done.4
  122.6 2.4 convolution_convert_fusion.3.refs_1_
  125.1 2.4 convolution_convert_fusion.1.refs_0_
  127.5 36.9 %reduce_blocks.3 = (f32[1024,512]{1,0:T(8,128)S(1)}, f32[256,512]{1,0:T(8,128)S(1)}, f32[64,64]{1,0:T(8,128)S(1)}) custom-call(bf16[1024,2048]{1,0:T(8,128)(2,1)S(1)} %convolution_convert_fusion.1.refs_0_, bf16[2048,512]{1,0:T(8,128)(2,1)S(1)} %convolution_convert_fusion.3.refs_1_, bf16[512,64]{1,0:T(8,128)(2,1)S(1)} %copy.17.refs_2_), custom_call_target="tpu_custom_call" | custom-call | tf_op jit(solution)/shard_map/reduce_blocks/pallas_call | solution.py:347
  164.4 3.4 %fusion.42 = (f32[512]{0:T(512)S(1)}, f32[512]{0:T(512)S(1)}, f32[1024,512]{1,0:T(8,128)}) fusion(f32[512]{0:T(512)S(1)} %fusion.34, f32[1024,512]{1,0:T(8,128)S(1)} %copy-done.6, f32[512]{0:T(512)S(1)} %get-tuple-element.59, f32[1024,512]{1,0:T(8,128)S(1)} %get-tuple-element.16, f32[512]{0:T(512)S(1)} %bitcast.122, f32[512]{0:T(512)S(1)} %bitcast.120), kind=kLoop, calls=%fused_computation.119 | loop fusion | flops 17300480 | bytes 6303744 | tf_op jit(solution)/shard_map/reduce_sum | solution.py:430
  167.9 6.5 %sum_pair.10 = f32[8,128]{1,0:T(8,128)S(1)} custom-call(f32[8,128]{1,0:T(8,128)S(1)} %reshape.246.x_ref), custom_call_target="tpu_custom_call" | custom-call | tf_op jit(solution)/shard_map/sum_pair/pallas_call | solution.py:67
  174.4 3.0 %multiply_convert_fusion.1 = bf16[1024,512]{1,0:T(8,128)(2,1)S(1)} fusion(f32[1024,512]{1,0:T(8,128)} %get-tuple-element.34, f32[1024,512]{1,0:T(8,128)} %copy-done.5, f32[512]{0:T(512)S(1)} %get-tuple-element.50, f32[512]{0:T(512)S(1)} %get-tuple-element.49, f32[512]{0:T(512)S(1)} %fusion.34, f32[512]{0:T(512)S(1)} %get-tuple-element.59, f32[512]{0:T(512)S(1)} %bitcast.123), kind=kLoop, calls=%fused_computation.33 | loop fusion | flops 4194304 | bytes 5253120 | tf_op jit(solution)/shard_map/convert_element_type | solution.py:436
  177.4 0.5 copy-done.2
  177.9 2.4 convolution_convert_fusion.2.refs_1_
  180.3 2.4 convolution_convert_fusion.refs_0_
  182.7 30.4 %reduce_blocks.4 = (f32[1024,512]{1,0:T(8,128)S(1)}, f32[256,512]{1,0:T(8,128)S(1)}) custom-call(bf16[1024,2048]{1,0:T(8,128)(2,1)S(1)} %convolution_convert_fusion.refs_0_, bf16[2048,512]{1,0:T(8,128)(2,1)S(1)} %convolution_convert_fusion.2.refs_1_), custom_call_target="tpu_custom_call" | custom-call | tf_op jit(solution)/shard_map/reduce_blocks/pallas_call | solution.py:347
  213.1 1.0 pad_maximum_fusion
  214.1 0.9 copy-done.8
  215.0 3.4 %fusion.41 = (f32[512]{0:T(512)S(1)}, f32[512]{0:T(512)S(1)}, f32[1024,512]{1,0:T(8,128)}) fusion(f32[512]{0:T(512)S(1)} %fusion.36, f32[1024,512]{1,0:T(8,128)S(1)} %copy-done.8, f32[512]{0:T(512)S(1)} %get-tuple-element.57, f32[1024,512]{1,0:T(8,128)S(1)} %get-tuple-element.17, f32[512]{0:T(512)S(1)} %bitcast.118, f32[512]{0:T(512)S(1)} %bitcast.116), kind=kLoop, calls=%fused_computation.118 | loop fusion | flops 17300480 | bytes 6303744 | tf_op jit(solution)/shard_map/reduce_sum | solution.py:430
  218.5 8.6 %sum_pair.11 = f32[8,128]{1,0:T(8,128)S(1)} custom-call(f32[8,128]{1,0:T(8,128)S(1)} %reshape.247.x_ref), custom_call_target="tpu_custom_call" | custom-call | tf_op jit(solution)/shard_map/sum_pair/pallas_call | solution.py:67
  227.1 3.6 %convolution_convert_fusion.4.refs_0_ = bf16[1024,512]{1,0:T(8,128)(2,1)S(1)} fusion(bf16[1024,1024]{1,0:T(8,128)(2,1)} %copy-done.10, f32[1024,512]{1,0:T(8,128)} %get-tuple-element.33, f32[1024,512]{1,0:T(8,128)S(1)} %copy-done.9, f32[512]{0:T(512)S(1)} %get-tuple-element.46, f32[512]{0:T(512)S(1)} %get-tuple-element.45, f32[512]{0:T(512)S(1)} %fusion.36, ...), kind=kOutput, calls=%fused_computation.62 | convolution fusion | flops 1078460416 | bytes 7350272 | tf_op jit(solution)/shard_map/dot_general | solution.py:393
  230.8 16.9 %reduce_blocks.5 = f32[128,512]{1,0:T(8,128)S(1)} custom-call(bf16[1024,512]{1,0:T(8,128)(2,1)S(1)} %convolution_convert_fusion.4.refs_0_), custom_call_target="tpu_custom_call" | custom-call | tf_op jit(solution)/shard_map/reduce_blocks/pallas_call | solution.py:347
  247.7 0.6 pad_maximum_fusion.2
  248.3 0.6 pad_maximum_fusion.1
  248.9 0.7 copy.20
  249.6 0.6 copy.21
  (38 shorter events, 0.3 us)
Async XLA Ops:
  0.6 10.0 %copy-start = (bf16[1024,512]{1,0:T(8,128)(2,1)S(1)}, bf16[1024,512]{1,0:T(8,128)(2,1)}, u32[]{:S(2)}) copy-start(bf16[1024,512]{1,0:T(8,128)(2,1)} %param.16) | copy-start | bytes 3145732
  10.6 1.4 copy-start.10
  12.0 10.0 %copy-start.7 = (f32[1024,512]{1,0:T(8,128)}, f32[1024,512]{1,0:T(8,128)S(1)}, u32[]{:S(2)}) copy-start(f32[1024,512]{1,0:T(8,128)S(1)} %get-tuple-element.64) | copy-start | bytes 6291460
  21.9 26.7 %copy-start.14 = (bf16[2,2048,512]{2,1,0:T(8,128)(2,1)S(1)}, bf16[2,2048,512]{2,1,0:T(8,128)(2,1)}, u32[]{:S(2)}) copy-start(bf16[2,2048,512]{2,1,0:T(8,128)(2,1)} %param.17) | copy-start | bytes 12582916
  48.7 2.4 copy-start.1
  51.1 34.0 %copy-start.5 = (f32[1024,512]{1,0:T(8,128)}, f32[1024,512]{1,0:T(8,128)S(1)}, u32[]{:S(2)}) copy-start(f32[1024,512]{1,0:T(8,128)S(1)} %get-tuple-element.65) | copy-start | bytes 6291460
  59.2 25.8 %copy-start.15 = (bf16[2,2048,512]{2,1,0:T(8,128)(2,1)S(1)}, bf16[2,2048,512]{2,1,0:T(8,128)(2,1)}, u32[]{:S(2)}) copy-start(bf16[2,2048,512]{2,1,0:T(8,128)(2,1)} %param.17) | copy-start | bytes 12582916
  85.0 3.7 %copy-start.3 = (bf16[1024,2048]{1,0:T(8,128)(2,1)}, bf16[1024,2048]{1,0:T(8,128)(2,1)S(1)}, u32[]{:S(2)}) copy-start(bf16[1024,2048]{1,0:T(8,128)(2,1)S(1)} %gather_columns.3) | copy-start | bytes 12582916
  85.1 10.4 %copy-start.13 = (f32[3,512]{1,0:T(4,128)S(1)}, f32[3,512]{1,0:T(4,128)}, u32[]{:S(2)}) copy-start(f32[3,512]{1,0:T(4,128)} %param.19) | copy-start | bytes 18436
  88.8 9.7 %copy-start.12 = (bf16[512,64]{0,1:T(8,128)(2,1)S(1)}, bf16[512,64]{0,1:T(8,128)(2,1)}, u32[]{:S(2)}) copy-start(bf16[512,64]{0,1:T(8,128)(2,1)} %param.18) | copy-start | bytes 196612
  95.4 11.2 %copy-start.11 = (f32[1024,64]{0,1:T(8,128)S(1)}, f32[1024,64]{0,1:T(8,128)}, u32[]{:S(2)}) copy-start(f32[1024,64]{0,1:T(8,128)} %param.21) | copy-start | bytes 786436
  119.2 3.5 %copy-start.4 = (bf16[1024,2048]{1,0:T(8,128)(2,1)S(1)}, bf16[1024,2048]{1,0:T(8,128)(2,1)}, u32[]{:S(2)}) copy-start(bf16[1024,2048]{1,0:T(8,128)(2,1)} %copy-done.3) | copy-start | bytes 12582916
  122.6 2.5 copy-start.16
  127.5 36.9 %copy-start.6 = (f32[1024,512]{1,0:T(8,128)S(1)}, f32[1024,512]{1,0:T(8,128)}, u32[]{:S(2)}) copy-start(f32[1024,512]{1,0:T(8,128)} %copy-done.5) | copy-start | bytes 6291460
  174.4 3.5 %copy-start.2 = (bf16[1024,2048]{1,0:T(8,128)(2,1)S(1)}, bf16[1024,2048]{1,0:T(8,128)(2,1)}, u32[]{:S(2)}) copy-start(bf16[1024,2048]{1,0:T(8,128)(2,1)} %copy-done.1) | copy-start | bytes 12582916
  177.9 2.5 copy-start.17
  213.1 2.0 copy-start.8
  215.0 12.1 %copy-start.9 = (f32[1024,512]{1,0:T(8,128)S(1)}, f32[1024,512]{1,0:T(8,128)}, u32[]{:S(2)}) copy-start(f32[1024,512]{1,0:T(8,128)} %copy-done.7) | copy-start | bytes 6291460

commit v4 on v3

--- a/solution.py
+++ b/solution.py
@@ -89,7 +89,7 @@
 
 VMEM_SPEC = pl.BlockSpec(memory_space=pltpu.VMEM)
 MESH_ID = pl.DeviceIdType.MESH
-CHUNKS = 4
+CHUNKS = 8
 
 
 def meet(targets):

time: 251 us -> 251 us (level)
  no operation moved by 1% of the time
where the time goes in v4:
time: 251 us
  Pallas kernels  189 us (75%)
  other arithmetic  29.2 us (12%)
  matrix products  26.3 us (10%)
  local copies, waits for them, and re-layouts  5.15 us (2%)
    pallas_call x3, Pallas kernels, reduce_blocks(): pl.pallas_call(functools.partial(reduce_kernel, 'dp', n, quad, count), ou...  84.5 us
    pallas_call x2, Pallas kernels, gather_columns(): pl.pallas_call(functools.partial(gather_kernel, axis), out_shape=jax.Shap...  52.7 us
    pallas_call x7, Pallas kernels, exchange_sum(): pl.pallas_call(functools.partial(exchange_kernel, axis, n), out_shape=jax...  51.7 us
    dot_general x4, matrix products, column_products(): return jnp.dot(left_rows.T, right_rows, preferred_element_type=jnp.float32)  8.81 us
    reduce_sum x2, other arithmetic, per_device(): jnp.sum(slope_a, axis=0)  6.85 us
    dot_general x2, matrix products, per_device(): jnp.dot(whole_input, w_mid[layer_at - 1], preferred_element_type=jnp.floa...  6.01 us
    convert_element_type x2, other arithmetic, per_device(): slope_z = (bn_gain[layer_at] * inverse * (slope_a - bias_sum / batch_tota...  5.93 us
    convert_element_type x3, other arithmetic, per_device(): current = mish_act(shifted).astype(jnp.bfloat16)  5.63 us

profile of v4, /device:TPU:0, one launch (start us, length us, event | category | flops | bytes accessed | tf_op | source)
XLA Modules:
  0.0 250.7 jit_solution(6633793685355567835)
XLA Ops:
  0.6 0.0 copy-start
  0.6 0.8 convert_element_type.71
  1.4 0.7 convert_element_type.73
  2.1 0.7 convert_element_type.72
  2.8 0.8 fusion.48
  3.6 0.8 fusion.47
  4.4 0.8 convert_divide_fusion
  5.2 5.4 %add_convert_fusion = bf16[1024,1024]{1,0:T(8,128)(2,1)S(1)} fusion(f32[1024]{0:T(1024)S(1)} %get-tuple-element.15, f32[1024]{0:T(1024)S(1)} %convert_element_type.73, f32[1024]{0:T(1024)S(1)} %get-tuple-element.14, f32[1024]{0:T(1024)S(1)} %convert_element_type.72, s32[1024]{0:T(1024)} %param.13, s32[1024]{0:T(1024)} %param.14, ...), kind=kLoop, calls=%fused_computation.2 | loop fusion | flops 28311552 | bytes 2138112 | tf_op jit(solution)/shard_map/convert_element_type | solution.py:30
  10.6 0.0 copy-done
  10.6 0.0 copy-start.10
  10.6 1.3 fusion.46
  11.9 0.1 copy-done.10
  12.0 8.6 %sum_pair.6 = f32[8,128]{1,0:T(8,128)S(1)} custom-call(f32[8,128]{1,0:T(8,128)S(1)} %reshape.242.x_ref), custom_call_target="tpu_custom_call" | custom-call | tf_op jit(solution)/shard_map/sum_pair/pallas_call | solution.py:67
  20.6 1.3 fusion.17.x_ref
  21.9 0.0 copy-done.7
  21.9 0.0 copy-start.14
  22.0 26.8 %gather_columns.2 = bf16[1024,2048]{1,0:T(8,128)(2,1)S(1)} custom-call(bf16[1024,512]{1,0:T(8,128)(2,1)S(1)} %fusion.17.x_ref), custom_call_target="tpu_custom_call" | custom-call | tf_op jit(solution)/shard_map/gather_columns/pallas_call | solution.py:154
  48.7 0.0 copy-done.14
  48.7 0.0 copy-start.1
  48.8 2.3 fusion.45
  51.1 0.0 copy-done.1
  51.1 0.0 copy-start.5
  51.1 6.6 %sum_pair.7 = f32[8,128]{1,0:T(8,128)S(1)} custom-call(f32[8,128]{1,0:T(8,128)S(1)} %reshape.243.x_ref), custom_call_target="tpu_custom_call" | custom-call | tf_op jit(solution)/shard_map/sum_pair/pallas_call | solution.py:67
  57.8 1.3 fusion.16.x_ref
  59.2 0.0 copy-start.15
  59.2 25.9 %gather_columns.3 = bf16[1024,2048]{1,0:T(8,128)(2,1)S(1)} custom-call(bf16[1024,512]{1,0:T(8,128)(2,1)S(1)} %fusion.16.x_ref), custom_call_target="tpu_custom_call" | custom-call | tf_op jit(solution)/shard_map/gather_columns/pallas_call | solution.py:154
  85.1 0.0 copy-done.5
  85.1 0.0 copy-done.15
  85.1 0.0 copy-start.13
  85.1 3.7 %fusion.44 = (f32[512]{0:T(512)S(1)}, f32[512]{0:T(512)S(1)}, f32[1024,512]{1,0:T(8,128)}) fusion(bf16[1024,2048]{1,0:T(8,128)(2,1)S(1)} %gather_columns.3, bf16[2,2048,512]{2,1,0:T(8,128)(2,1)S(1)} %copy-done.15), kind=kOutput, calls=%fused_computation.121 | convolution fusion | flops 2149055488 | bytes 8392704 | tf_op jit(solution)/shard_map/dot_general | solution.py:410
  88.8 0.0 copy-done.3
  88.8 6.6 %sum_pair.8 = f32[8,128]{1,0:T(8,128)S(1)} custom-call(f32[8,128]{1,0:T(8,128)S(1)} %reshape.244.x_ref), custom_call_target="tpu_custom_call" | custom-call | tf_op jit(solution)/shard_map/sum_pair/pallas_call | solution.py:67
  95.5 0.0 copy-start.11
  95.5 3.0 %fusion.15 = bf16[1024,512]{1,0:T(8,128)(2,1)S(1)} fusion(f32[1024,512]{1,0:T(8,128)} %get-tuple-element.66, f32[512]{0:T(512)S(1)} %bitcast.127, f32[512]{0:T(512)S(1)} %fusion.32, f32[512]{0:T(512)S(1)} %get-tuple-element.61, f32[512]{0:T(512)S(1)} %bitcast.125), kind=kLoop, calls=%fused_computation.55 | loop fusion | flops 9437184 | bytes 3153920 | tf_op jit(solution)/shard_map/convert_element_type | solution.py:414
  98.5 0.4 fusion.22.x_ref
  98.9 7.8 %sum_output.1 = f32[64,1024]{1,0:T(8,128)S(1)} custom-call(bf16[64,1024]{1,0:T(8,128)(2,1)S(1)} %fusion.22.x_ref), custom_call_target="tpu_custom_call" | custom-call | tf_op jit(solution)/shard_map/sum_output/pallas_call | solution.py:67
  106.8 0.3 convolution_convert_fusion.6
  107.1 0.1 copy.17.refs_2_
  107.2 5.1 %fusion.43 = (f32[512]{0:T(512)S(1)}, f32[512]{0:T(512)S(1)}, f32[1024,512]{1,0:T(8,128)}) fusion(f32[512]{0:T(512)S(1)} %fusion.32, f32[1024,512]{1,0:T(8,128)} %get-tuple-element.66, f32[512]{0:T(512)S(1)} %get-tuple-element.61, f32[512]{0:T(512)S(1)} %bitcast.128, f32[512]{0:T(512)S(1)} %bitcast.126, bf16[1024,64]{0,1:T(8,128)(2,1)S(1)} %fusion.30, ...), kind=kOutput, calls=%fused_computation.120 | convolution fusion | flops 84409344 | bytes 4403200 | tf_op jit(solution)/shard_map/dot_general | solution.py:421
  112.3 6.9 %sum_pair.9 = f32[8,128]{1,0:T(8,128)S(1)} custom-call(f32[8,128]{1,0:T(8,128)S(1)} %reshape.245.x_ref), custom_call_target="tpu_custom_call" | custom-call | tf_op jit(solution)/shard_map/sum_pair/pallas_call | solution.py:67
  119.3 3.0 %multiply_convert_fusion.2 = bf16[1024,512]{1,0:T(8,128)(2,1)S(1)} fusion(f32[1024,512]{1,0:T(8,128)} %get-tuple-element.67, f32[1024,512]{1,0:T(8,128)} %get-tuple-element.66, f32[512]{0:T(512)S(1)} %get-tuple-element.54, f32[512]{0:T(512)S(1)} %get-tuple-element.53, f32[512]{0:T(512)S(1)} %fusion.32, f32[512]{0:T(512)S(1)} %get-tuple-element.61, ...), kind=kLoop, calls=%fused_computation.38 | loop fusion | flops 4194304 | bytes 5253120 | tf_op jit(solution)/shard_map/convert_element_type | solution.py:436
  122.3 0.5 copy-done.4
  122.7 2.4 convolution_convert_fusion.3.refs_1_
  125.2 2.4 convolution_convert_fusion.1.refs_0_
  127.6 37.1 %reduce_blocks.3 = (f32[1024,512]{1,0:T(8,128)S(1)}, f32[256,512]{1,0:T(8,128)S(1)}, f32[64,64]{1,0:T(8,128)S(1)}) custom-call(bf16[1024,2048]{1,0:T(8,128)(2,1)S(1)} %convolution_convert_fusion.1.refs_0_, bf16[2048,512]{1,0:T(8,128)(2,1)S(1)} %convolution_convert_fusion.3.refs_1_, bf16[512,64]{1,0:T(8,128)(2,1)S(1)} %copy.17.refs_2_), custom_call_target="tpu_custom_call" | custom-call | tf_op jit(solution)/shard_map/reduce_blocks/pallas_call | solution.py:347
  164.7 3.4 %fusion.42 = (f32[512]{0:T(512)S(1)}, f32[512]{0:T(512)S(1)}, f32[1024,512]{1,0:T(8,128)}) fusion(f32[512]{0:T(512)S(1)} %fusion.34, f32[1024,512]{1,0:T(8,128)S(1)} %copy-done.6, f32[512]{0:T(512)S(1)} %get-tuple-element.59, f32[1024,512]{1,0:T(8,128)S(1)} %get-tuple-element.16, f32[512]{0:T(512)S(1)} %bitcast.122, f32[512]{0:T(512)S(1)} %bitcast.120), kind=kLoop, calls=%fused_computation.119 | loop fusion | flops 17300480 | bytes 6303744 | tf_op jit(solution)/shard_map/reduce_sum | solution.py:430
  168.1 6.5 %sum_pair.10 = f32[8,128]{1,0:T(8,128)S(1)} custom-call(f32[8,128]{1,0:T(8,128)S(1)} %reshape.246.x_ref), custom_call_target="tpu_custom_call" | custom-call | tf_op jit(solution)/shard_map/sum_pair/pallas_call | solution.py:67
  174.7 3.0 %multiply_convert_fusion.1 = bf16[1024,512]{1,0:T(8,128)(2,1)S(1)} fusion(f32[1024,512]{1,0:T(8,128)} %get-tuple-element.34, f32[1024,512]{1,0:T(8,128)} %copy-done.5, f32[512]{0:T(512)S(1)} %get-tuple-element.50, f32[512]{0:T(512)S(1)} %get-tuple-element.49, f32[512]{0:T(512)S(1)} %fusion.34, f32[512]{0:T(512)S(1)} %get-tuple-element.59, f32[512]{0:T(512)S(1)} %bitcast.123), kind=kLoop, calls=%fused_computation.33 | loop fusion | flops 4194304 | bytes 5253120 | tf_op jit(solution)/shard_map/convert_element_type | solution.py:436
  177.7 0.5 copy-done.2
  178.1 2.4 convolution_convert_fusion.2.refs_1_
  180.6 0.0 copy-done.17
  180.6 2.4 convolution_convert_fusion.refs_0_
  183.0 30.5 %reduce_blocks.4 = (f32[1024,512]{1,0:T(8,128)S(1)}, f32[256,512]{1,0:T(8,128)S(1)}) custom-call(bf16[1024,2048]{1,0:T(8,128)(2,1)S(1)} %convolution_convert_fusion.refs_0_, bf16[2048,512]{1,0:T(8,128)(2,1)S(1)} %convolution_convert_fusion.2.refs_1_), custom_call_target="tpu_custom_call" | custom-call | tf_op jit(solution)/shard_map/reduce_blocks/pallas_call | solution.py:347
  213.5 1.0 pad_maximum_fusion
  214.6 0.9 copy-done.8
  215.5 3.4 %fusion.41 = (f32[512]{0:T(512)S(1)}, f32[512]{0:T(512)S(1)}, f32[1024,512]{1,0:T(8,128)}) fusion(f32[512]{0:T(512)S(1)} %fusion.36, f32[1024,512]{1,0:T(8,128)S(1)} %copy-done.8, f32[512]{0:T(512)S(1)} %get-tuple-element.57, f32[1024,512]{1,0:T(8,128)S(1)} %get-tuple-element.17, f32[512]{0:T(512)S(1)} %bitcast.118, f32[512]{0:T(512)S(1)} %bitcast.116), kind=kLoop, calls=%fused_computation.118 | loop fusion | flops 17300480 | bytes 6303744 | tf_op jit(solution)/shard_map/reduce_sum | solution.py:430
  218.9 8.7 %sum_pair.11 = f32[8,128]{1,0:T(8,128)S(1)} custom-call(f32[8,128]{1,0:T(8,128)S(1)} %reshape.247.x_ref), custom_call_target="tpu_custom_call" | custom-call | tf_op jit(solution)/shard_map/sum_pair/pallas_call | solution.py:67
  227.6 0.0 copy-done.9
  227.6 3.6 %convolution_convert_fusion.4.refs_0_ = bf16[1024,512]{1,0:T(8,128)(2,1)S(1)} fusion(bf16[1024,1024]{1,0:T(8,128)(2,1)} %copy-done.10, f32[1024,512]{1,0:T(8,128)} %get-tuple-element.33, f32[1024,512]{1,0:T(8,128)S(1)} %copy-done.9, f32[512]{0:T(512)S(1)} %get-tuple-element.46, f32[512]{0:T(512)S(1)} %get-tuple-element.45, f32[512]{0:T(512)S(1)} %fusion.36, ...), kind=kOutput, calls=%fused_computation.62 | convolution fusion | flops 1078460416 | bytes 7350272 | tf_op jit(solution)/shard_map/dot_general | solution.py:393
  231.3 16.9 %reduce_blocks.5 = f32[128,512]{1,0:T(8,128)S(1)} custom-call(bf16[1024,512]{1,0:T(8,128)(2,1)S(1)} %convolution_convert_fusion.4.refs_0_), custom_call_target="tpu_custom_call" | custom-call | tf_op jit(solution)/shard_map/reduce_blocks/pallas_call | solution.py:347
  248.2 0.6 pad_maximum_fusion.2
  248.8 0.6 pad_maximum_fusion.1
  249.4 0.7 copy.20
  250.1 0.6 copy.21
  (38 shorter events, 0.3 us)
Async XLA Ops:
  0.6 10.0 %copy-start = (bf16[1024,512]{1,0:T(8,128)(2,1)S(1)}, bf16[1024,512]{1,0:T(8,128)(2,1)}, u32[]{:S(2)}) copy-start(bf16[1024,512]{1,0:T(8,128)(2,1)} %param.16) | copy-start | bytes 3145732
  10.6 1.4 copy-start.10
  12.0 10.0 %copy-start.7 = (f32[1024,512]{1,0:T(8,128)}, f32[1024,512]{1,0:T(8,128)S(1)}, u32[]{:S(2)}) copy-start(f32[1024,512]{1,0:T(8,128)S(1)} %get-tuple-element.64) | copy-start | bytes 6291460
  21.9 26.8 %copy-start.14 = (bf16[2,2048,512]{2,1,0:T(8,128)(2,1)S(1)}, bf16[2,2048,512]{2,1,0:T(8,128)(2,1)}, u32[]{:S(2)}) copy-start(bf16[2,2048,512]{2,1,0:T(8,128)(2,1)} %param.17) | copy-start | bytes 12582916
  48.7 2.4 copy-start.1
  51.1 34.0 %copy-start.5 = (f32[1024,512]{1,0:T(8,128)}, f32[1024,512]{1,0:T(8,128)S(1)}, u32[]{:S(2)}) copy-start(f32[1024,512]{1,0:T(8,128)S(1)} %get-tuple-element.65) | copy-start | bytes 6291460
  59.2 25.9 %copy-start.15 = (bf16[2,2048,512]{2,1,0:T(8,128)(2,1)S(1)}, bf16[2,2048,512]{2,1,0:T(8,128)(2,1)}, u32[]{:S(2)}) copy-start(bf16[2,2048,512]{2,1,0:T(8,128)(2,1)} %param.17) | copy-start | bytes 12582916
  85.1 3.7 %copy-start.3 = (bf16[1024,2048]{1,0:T(8,128)(2,1)}, bf16[1024,2048]{1,0:T(8,128)(2,1)S(1)}, u32[]{:S(2)}) copy-start(bf16[1024,2048]{1,0:T(8,128)(2,1)S(1)} %gather_columns.3) | copy-start | bytes 12582916
  85.1 10.4 %copy-start.13 = (f32[3,512]{1,0:T(4,128)S(1)}, f32[3,512]{1,0:T(4,128)}, u32[]{:S(2)}) copy-start(f32[3,512]{1,0:T(4,128)} %param.19) | copy-start | bytes 18436
  88.8 9.7 %copy-start.12 = (bf16[512,64]{0,1:T(8,128)(2,1)S(1)}, bf16[512,64]{0,1:T(8,128)(2,1)}, u32[]{:S(2)}) copy-start(bf16[512,64]{0,1:T(8,128)(2,1)} %param.18) | copy-start | bytes 196612
  95.5 11.2 %copy-start.11 = (f32[1024,64]{0,1:T(8,128)S(1)}, f32[1024,64]{0,1:T(8,128)}, u32[]{:S(2)}) copy-start(f32[1024,64]{0,1:T(8,128)} %param.21) | copy-start | bytes 786436
  119.3 3.5 %copy-start.4 = (bf16[1024,2048]{1,0:T(8,128)(2,1)S(1)}, bf16[1024,2048]{1,0:T(8,128)(2,1)}, u32[]{:S(2)}) copy-start(bf16[1024,2048]{1,0:T(8,128)(2,1)} %copy-done.3) | copy-start | bytes 12582916
  122.7 2.5 copy-start.16
  127.6 37.1 %copy-start.6 = (f32[1024,512]{1,0:T(8,128)S(1)}, f32[1024,512]{1,0:T(8,128)}, u32[]{:S(2)}) copy-start(f32[1024,512]{1,0:T(8,128)} %copy-done.5) | copy-start | bytes 6291460
  174.7 3.5 %copy-start.2 = (bf16[1024,2048]{1,0:T(8,128)(2,1)S(1)}, bf16[1024,2048]{1,0:T(8,128)(2,1)}, u32[]{:S(2)}) copy-start(bf16[1024,2048]{1,0:T(8,128)(2,1)} %copy-done.1) | copy-start | bytes 12582916
  178.1 2.5 copy-start.17
  213.5 2.0 copy-start.8
  215.5 12.1 %copy-start.9 = (f32[1024,512]{1,0:T(8,128)S(1)}, f32[1024,512]{1,0:T(8,128)}, u32[]{:S(2)}) copy-start(f32[1024,512]{1,0:T(8,128)} %copy-done.7) | copy-start | bytes 6291460
